TPU v7x, 128 devices: a whole 4x4x4 slice. The times are simulated.
128 devices in a mesh: patch: 16 (over y, z), col: 8 (over x, core).
Axes of the slice: x: 4, y: 4, z: 4, core: 2. Of those that a mesh axis runs over, the one named last changes fastest.
Arguments:
- contributions: float32 [8192, 128, 128], P(('patch', 'col')), may hold values from -0.21875 to 0.21875
- targets: int32 [8192, 2], P(('patch', 'col')), may hold values from 0 to 127, as said below
- counts: int32 [128], P(('patch', 'col')), may hold values from 48 to 64, as said below
- pivot: int32 [128], replicated, may hold values from 0 to 127, as said below
- fill_draw: int32 [128, 128], replicated, may hold values 0 or 1
- regular: float32 [16384], P('patch'), may hold values from 1.5 to 3
Outputs:
- factor_panels: float32 [16384, 1024], P('patch')
- schur: float32 [16, 8, 16384, 128], P(None, 'col', 'patch')
Inputs may be any that keep to these rules, and one draw needn't show every extreme that they name: `targets`: under pivot, each contribution's pair lands at position (r, c) with r >= c after ordering; its owner is device (r // 8) * 8 + c % 8 of patch+col. Every slot of one device, live or not, has a different owner, so a device sends at most one block to each owner; one owner receives a block from every device. `pivot`: A permutation: each position once. `counts`: some device has all its slots live.
All inputs are finite; a program needn't handle non-finite values.
Results may differ from a plain program's by a relative error of at most 0.0001.
Values sent between devices are 32-bit elements; how exact they have to be, the bound alone decides.
A program may use at most 256 MiB of HBM per device.

v0:
```python
import jax
import jax.numpy as jnp
from jax import lax
from jax.sharding import PartitionSpec as P

K = 8


HIGH = lax.Precision.HIGHEST


def broadcast(block, axis, holder):
    block = jnp.where(lax.axis_index(axis) == holder, block, jnp.zeros_like(block))
    return lax.psum(block, axis)


def body(contributions, targets, counts, pivot, fill_draw, regular):
    width = contributions.shape[1]
    npatch = lax.axis_size("patch")
    ncol = lax.axis_size("col")
    ndevice = npatch * ncol
    nblock = pivot.shape[0]
    rowblk = regular.shape[0] // width
    colslots = nblock // ncol
    slots = contributions.shape[0]
    patch_id = lax.axis_index("patch")
    col_id = lax.axis_index("col")
    pos_first = pivot[targets[:, 0]]
    pos_second = pivot[targets[:, 1]]
    upper_pos = jnp.maximum(pos_first, pos_second)
    lower_pos = jnp.minimum(pos_first, pos_second)
    placed = jnp.where(
        (pos_first < pos_second)[:, None, None], jnp.swapaxes(contributions, 1, 2), contributions
    )
    live = jnp.arange(slots, dtype=jnp.int32) < counts[0]
    owner = upper_pos // rowblk * ncol + lower_pos % ncol
    select = (owner[:, None] == jnp.arange(ndevice, dtype=jnp.int32)[None, :]) & live[:, None]
    outgoing = jnp.einsum("ed,eab->dab", select.astype(jnp.float32), placed, precision=HIGH)
    place_code = upper_pos % rowblk * colslots + lower_pos // ncol
    meta = jnp.stack(
        [
            jnp.sum(jnp.where(select, place_code[:, None], 0), 0),
            jnp.sum(select.astype(jnp.int32), 0),
        ],
        1,
    )
    got_blocks, got_meta = (
        lax.all_to_all(outgoing, ("patch", "col"), split_axis=0, concat_axis=0, tiled=True),
        lax.all_to_all(meta, ("patch", "col"), split_axis=0, concat_axis=0, tiled=True),
    )
    places = jnp.arange(rowblk * colslots, dtype=jnp.int32)
    place_table = (
        (got_meta[:, 0][:, None] == places[None, :]) & (got_meta[:, 1][:, None] > 0)
    ).astype(jnp.float32)
    matrix = jnp.einsum("dq,dab->qab", place_table, got_blocks, precision=HIGH).reshape(
        rowblk, colslots, width, width
    )
    grow = patch_id * rowblk + jnp.arange(rowblk, dtype=jnp.int32)
    gcol = jnp.arange(colslots, dtype=jnp.int32) * ncol + col_id
    on_diagonal = grow[:, None] == gcol[None, :]
    symmetric = 0.5 * (matrix + jnp.swapaxes(matrix, 2, 3))
    shift = jnp.eye(width, dtype=jnp.float32)[None] * regular.reshape(rowblk, 1, width)
    matrix = jnp.where(on_diagonal[:, :, None, None], symmetric + shift[:, None], matrix)
    drawn = fill_draw.astype(jnp.float32)
    pattern = jnp.maximum(jnp.maximum(drawn, drawn.T), jnp.eye(nblock, dtype=jnp.float32))
    band = lax.dynamic_slice_in_dim(pattern, patch_id * rowblk, rowblk, 0).reshape(
        rowblk, colslots, ncol
    )
    local_fill = lax.dynamic_index_in_dim(band, col_id, 2, keepdims=False)
    weight = local_fill * (grow[:, None] >= gcol[None, :]).astype(jnp.float32)
    identity = jnp.eye(width, dtype=jnp.float32)
    factor_rows = []
    column_rows = []
    for kblock in range(K):
        slot = kblock // ncol
        owner_col = kblock % ncol
        root_patch = kblock // rowblk
        within = kblock % rowblk
        column = matrix[:, slot]
        pivot_block = broadcast(column[within], "patch", root_patch)
        pivot_block = jnp.where(col_id == owner_col, pivot_block, identity)
        chol = jnp.linalg.cholesky(pivot_block)
        stacked = column.transpose(2, 0, 1).reshape(width, rowblk * width)
        solved = lax.linalg.triangular_solve(chol, stacked, left_side=True, lower=True)
        rows_l = solved.reshape(width, rowblk, width).transpose(1, 2, 0)
        rows_l = jnp.where(
            (grow > kblock)[:, None, None],
            rows_l,
            jnp.where((grow == kblock)[:, None, None], chol[None], jnp.zeros_like(rows_l)),
        )
        rows_l = broadcast(rows_l, "col", owner_col)
        picked = lax.dynamic_index_in_dim(
            rows_l.reshape(rowblk // ncol, ncol, width, width), col_id, 1, keepdims=False
        )
        cols_l = lax.all_gather(picked, "patch", axis=0, tiled=True)
        factor_rows.append(rows_l)
        column_rows.append(cols_l)
        update = jnp.einsum("rab,scb->rsac", rows_l, cols_l, precision=HIGH)
        mask = weight * (gcol > kblock).astype(jnp.float32)[None, :]
        matrix = matrix - mask[:, :, None, None] * update
    keep = (grow[:, None] >= gcol[None, :]) & (gcol >= K)[None, :]
    schur = jnp.where(keep[:, :, None, None], matrix, 0.0)
    schur = schur.transpose(1, 0, 2, 3).reshape(colslots, 1, rowblk * width, width)
    factor_panels = (
        jnp.stack(factor_rows, 1).transpose(0, 2, 1, 3).reshape(rowblk * width, K * width)
    )
    return (factor_panels, schur)


def solution(mesh):
    in_specs = (
        P(("patch", "col"), None, None),
        P(("patch", "col"), None),
        P(("patch", "col")),
        P(),
        P(),
        P("patch"),
    )
    out_specs = (P("patch", None), P(None, "col", "patch", None))
    return jax.shard_map(body, mesh=mesh, in_specs=in_specs, out_specs=out_specs, check_vma=False)
```

profile of v0, /device:TPU:24, one launch (start us, length us, event | category | flops | bytes accessed | tf_op | source)
XLA Modules:
  0.0 2016.4 jit_solution(237663633635613630)
XLA Ops:
  56.3 97.8 %all-to-all-done.1 = f32[128,128,128]{2,1,0:T(8,128)} async-done(((f32[128,128,128]{2,1,0:T(8,128)}), f32[128,128,128]{2,1,0:T(8,128)}, u32[]{:S(2)}, u32[]{:S(2)}) %all-to-all-start.1) | async-done | bytes 8388640 | tf_op jit(solution)/shard_map/all_to_all | solution.py:48
  154.1 15.6 fusion.13
  195.2 85.7 %all-reduce.17.cloned.1.call-done = f32[128,128]{0,1:T(8,128)} async-done(((f32[128,128]{0,1:T(8,128)}), f32[128,128]{0,1:T(8,128)}) %all-reduce.17.cloned.1.call-update) | async-done | bytes 65552 | tf_op jit(solution)/shard_map/psum | solution.py:14
  282.7 11.7 cholesky.134
  307.2 59.0 %all-reduce.19.cloned.1.call-done = f32[8,128,128]{2,1,0:T(8,128)} async-done(((f32[8,128,128]{2,1,0:T(8,128)}), f32[8,128,128]{2,1,0:T(8,128)}) %all-reduce.19.cloned.1.call-update) | async-done | bytes 524304 | tf_op jit(solution)/shard_map/psum | solution.py:14
  368.2 42.2 %all-gather.9.cloned.1.call-done = f32[16,128,128]{2,1,0:T(8,128)} async-done(((f32[1,128,128]{2,1,0:T(8,128)}), f32[16,128,128]{2,1,0:T(8,128)}) %all-gather.9.cloned.1.call-update) | async-done | bytes 1048592 | tf_op jit(solution)/shard_map/all_gather | solution.py:95
  426.0 80.0 %all-reduce.21.cloned.1.call-done = f32[128,128]{0,1:T(8,128)} async-done(((f32[128,128]{0,1:T(8,128)}), f32[128,128]{0,1:T(8,128)}) %all-reduce.21.cloned.1.call-update) | async-done | bytes 65552 | tf_op jit(solution)/shard_map/psum | solution.py:14
  506.1 11.7 cholesky.145
  530.6 60.7 %all-reduce.23.cloned.1.call-done = f32[8,128,128]{2,1,0:T(8,128)} async-done(((f32[8,128,128]{2,1,0:T(8,128)}), f32[8,128,128]{2,1,0:T(8,128)}) %all-reduce.23.cloned.1.call-update) | async-done | bytes 524304 | tf_op jit(solution)/shard_map/psum | solution.py:14
  592.9 42.6 %all-gather.11.cloned.1.call-done = f32[16,128,128]{2,1,0:T(8,128)} async-done(((f32[1,128,128]{2,1,0:T(8,128)}), f32[16,128,128]{2,1,0:T(8,128)}) %all-gather.11.cloned.1.call-update) | async-done | bytes 1048592 | tf_op jit(solution)/shard_map/all_gather | solution.py:95
  650.7 80.0 %all-reduce.25.cloned.1.call-done = f32[128,128]{0,1:T(8,128)} async-done(((f32[128,128]{0,1:T(8,128)}), f32[128,128]{0,1:T(8,128)}) %all-reduce.25.cloned.1.call-update) | async-done | bytes 65552 | tf_op jit(solution)/shard_map/psum | solution.py:14
  730.9 11.7 cholesky.156
  755.3 60.9 %all-reduce.27.cloned.1.call-done = f32[8,128,128]{2,1,0:T(8,128)} async-done(((f32[8,128,128]{2,1,0:T(8,128)}), f32[8,128,128]{2,1,0:T(8,128)}) %all-reduce.27.cloned.1.call-update) | async-done | bytes 524304 | tf_op jit(solution)/shard_map/psum | solution.py:14
  817.8 42.7 %all-gather.13.cloned.1.call-done = f32[16,128,128]{2,1,0:T(8,128)} async-done(((f32[1,128,128]{2,1,0:T(8,128)}), f32[16,128,128]{2,1,0:T(8,128)}) %all-gather.13.cloned.1.call-update) | async-done | bytes 1048592 | tf_op jit(solution)/shard_map/all_gather | solution.py:95
  875.8 80.0 %all-reduce.29.cloned.1.call-done = f32[128,128]{0,1:T(8,128)} async-done(((f32[128,128]{0,1:T(8,128)}), f32[128,128]{0,1:T(8,128)}) %all-reduce.29.cloned.1.call-update) | async-done | bytes 65552 | tf_op jit(solution)/shard_map/psum | solution.py:14
  956.0 11.7 cholesky.167
  980.5 60.7 %all-reduce.31.cloned.1.call-done = f32[8,128,128]{2,1,0:T(8,128)} async-done(((f32[8,128,128]{2,1,0:T(8,128)}), f32[8,128,128]{2,1,0:T(8,128)}) %all-reduce.31.cloned.1.call-update) | async-done | bytes 524304 | tf_op jit(solution)/shard_map/psum | solution.py:14
  1042.7 42.6 %all-gather.15.cloned.1.call-done = f32[16,128,128]{2,1,0:T(8,128)} async-done(((f32[1,128,128]{2,1,0:T(8,128)}), f32[16,128,128]{2,1,0:T(8,128)}) %all-gather.15.cloned.1.call-update) | async-done | bytes 1048592 | tf_op jit(solution)/shard_map/all_gather | solution.py:95
  1100.8 80.0 %all-reduce.33.cloned.1.call-done = f32[128,128]{0,1:T(8,128)} async-done(((f32[128,128]{0,1:T(8,128)}), f32[128,128]{0,1:T(8,128)}) %all-reduce.33.cloned.1.call-update) | async-done | bytes 65552 | tf_op jit(solution)/shard_map/psum | solution.py:14
  1205.4 62.4 %all-reduce.35.cloned.1.call-done = f32[8,128,128]{2,1,0:T(8,128)} async-done(((f32[8,128,128]{2,1,0:T(8,128)}), f32[8,128,128]{2,1,0:T(8,128)}) %all-reduce.35.cloned.1.call-update) | async-done | bytes 524304 | tf_op jit(solution)/shard_map/psum | solution.py:14
  1269.4 42.6 %all-gather.17.cloned.1.call-done = f32[16,128,128]{2,1,0:T(8,128)} async-done(((f32[1,128,128]{2,1,0:T(8,128)}), f32[16,128,128]{2,1,0:T(8,128)}) %all-gather.17.cloned.1.call-update) | async-done | bytes 1048592 | tf_op jit(solution)/shard_map/all_gather | solution.py:95
  1327.2 80.0 %all-reduce.37.cloned.1.call-done = f32[128,128]{0,1:T(8,128)} async-done(((f32[128,128]{0,1:T(8,128)}), f32[128,128]{0,1:T(8,128)}) %all-reduce.37.cloned.1.call-update) | async-done | bytes 65552 | tf_op jit(solution)/shard_map/psum | solution.py:14
  1431.9 60.6 %all-reduce.39.cloned.1.call-done = f32[8,128,128]{2,1,0:T(8,128)} async-done(((f32[8,128,128]{2,1,0:T(8,128)}), f32[8,128,128]{2,1,0:T(8,128)}) %all-reduce.39.cloned.1.call-update) | async-done | bytes 524304 | tf_op jit(solution)/shard_map/psum | solution.py:14
  1494.1 42.6 %all-gather.19.cloned.1.call-done = f32[16,128,128]{2,1,0:T(8,128)} async-done(((f32[1,128,128]{2,1,0:T(8,128)}), f32[16,128,128]{2,1,0:T(8,128)}) %all-gather.19.cloned.1.call-update) | async-done | bytes 1048592 | tf_op jit(solution)/shard_map/all_gather | solution.py:95
  1552.0 80.0 %all-reduce.41.cloned.1.call-done = f32[128,128]{0,1:T(8,128)} async-done(((f32[128,128]{0,1:T(8,128)}), f32[128,128]{0,1:T(8,128)}) %all-reduce.41.cloned.1.call-update) | async-done | bytes 65552 | tf_op jit(solution)/shard_map/psum | solution.py:14
  1656.6 62.1 %all-reduce.43.cloned.1.call-done = f32[8,128,128]{2,1,0:T(8,128)} async-done(((f32[8,128,128]{2,1,0:T(8,128)}), f32[8,128,128]{2,1,0:T(8,128)}) %all-reduce.43.cloned.1.call-update) | async-done | bytes 524304 | tf_op jit(solution)/shard_map/psum | solution.py:14
  1720.3 42.7 %all-gather.21.cloned.1.call-done = f32[16,128,128]{2,1,0:T(8,128)} async-done(((f32[1,128,128]{2,1,0:T(8,128)}), f32[16,128,128]{2,1,0:T(8,128)}) %all-gather.21.cloned.1.call-update) | async-done | bytes 1048592 | tf_op jit(solution)/shard_map/all_gather | solution.py:95
  1781.2 77.4 %all-reduce.45.cloned.1.call-done = f32[128,128]{0,1:T(8,128)} async-done(((f32[128,128]{0,1:T(8,128)}), f32[128,128]{0,1:T(8,128)}) %all-reduce.45.cloned.1.call-update) | async-done | bytes 65552 | tf_op jit(solution)/shard_map/psum | solution.py:14
  1858.7 11.7 cholesky.211
  1884.3 60.5 %all-reduce.47.cloned.1.call-done = f32[8,128,128]{2,1,0:T(8,128)} async-done(((f32[8,128,128]{2,1,0:T(8,128)}), f32[8,128,128]{2,1,0:T(8,128)}) %all-reduce.47.cloned.1.call-update) | async-done | bytes 524304 | tf_op jit(solution)/shard_map/psum | solution.py:14
  1954.2 34.2 %all-gather.23.cloned.1.call-done = f32[16,128,128]{2,1,0:T(8,128)} async-done(((f32[1,128,128]{2,1,0:T(8,128)}), f32[16,128,128]{2,1,0:T(8,128)}) %all-gather.23.cloned.1.call-update) | async-done | bytes 1048592 | tf_op jit(solution)/shard_map/all_gather | solution.py:95
  1988.4 11.7 fusion.2
  (257 shorter events, 354.4 us)
Async XLA Ops:
  11.1 34.3 %all-to-all-start = ((s32[128,1,2]{2,1,0:T(1,128)}), s32[128,1,2]{2,1,0:T(1,128)S(1)}, u32[]{:S(2)}, u32[]{:S(2)}) async-start(s32[128,1,2]{2,1,0:T(1,128)} %copy.161), calls=%async_computation | async-start | bytes 131072 | tf_op jit(solution)/shard_map/all_to_all | solution.py:49
  45.3 108.8 %all-to-all-start.1 = ((f32[128,128,128]{2,1,0:T(8,128)}), f32[128,128,128]{2,1,0:T(8,128)}, u32[]{:S(2)}, u32[]{:S(2)}) async-start(f32[128,128,128]{2,1,0:T(8,128)} %copy.164), calls=%async_computation.1 | async-start | bytes 16777216 | tf_op jit(solution)/shard_map/all_to_all | solution.py:48
  55.6 225.3 %all-reduce.17.cloned.1.call-start = ((), (), s32[]{:S(2)}) async-start(), calls=%async_computation.2 | async-start | bytes 131072 | tf_op jit(solution)/shard_map/psum | solution.py:14
  179.2 188.5 %copy-start.17 = (s32[128,128]{1,0:T(8,128)S(1)}, s32[128,128]{1,0:T(8,128)}, u32[]{:S(2)}) copy-start(s32[128,128]{1,0:T(8,128)} %param.13) | copy-start | bytes 196612
  193.8 172.3 %all-reduce.19.cloned.1.call-start = ((), (), s32[]{:S(2)}) async-start(), calls=%async_computation.3 | async-start | bytes 1048576 | tf_op jit(solution)/shard_map/psum | solution.py:14
  307.2 103.3 %all-gather.9.cloned.1.call-start = ((), (), s32[]{:S(2)}) async-start(), calls=%async_computation.4 | async-start | bytes 1114112 | tf_op jit(solution)/shard_map/all_gather | solution.py:95
  367.7 138.3 %all-reduce.21.cloned.1.call-start = ((), (), s32[]{:S(2)}) async-start(), calls=%async_computation.5 | async-start | bytes 131072 | tf_op jit(solution)/shard_map/psum | solution.py:14
  424.6 166.7 %all-reduce.23.cloned.1.call-start = ((), (), s32[]{:S(2)}) async-start(), calls=%async_computation.6 | async-start | bytes 1048576 | tf_op jit(solution)/shard_map/psum | solution.py:14
  530.5 104.9 %all-gather.11.cloned.1.call-start = ((), (), s32[]{:S(2)}) async-start(), calls=%async_computation.7 | async-start | bytes 1114112 | tf_op jit(solution)/shard_map/all_gather | solution.py:95
  592.8 137.9 %all-reduce.25.cloned.1.call-start = ((), (), s32[]{:S(2)}) async-start(), calls=%async_computation.8 | async-start | bytes 131072 | tf_op jit(solution)/shard_map/psum | solution.py:14
  649.4 166.8 %all-reduce.27.cloned.1.call-start = ((), (), s32[]{:S(2)}) async-start(), calls=%async_computation.9 | async-start | bytes 1048576 | tf_op jit(solution)/shard_map/psum | solution.py:14
  755.3 105.2 %all-gather.13.cloned.1.call-start = ((), (), s32[]{:S(2)}) async-start(), calls=%async_computation.10 | async-start | bytes 1114112 | tf_op jit(solution)/shard_map/all_gather | solution.py:95
  817.7 138.1 %all-reduce.29.cloned.1.call-start = ((), (), s32[]{:S(2)}) async-start(), calls=%async_computation.11 | async-start | bytes 131072 | tf_op jit(solution)/shard_map/psum | solution.py:14
  874.5 166.7 %all-reduce.31.cloned.1.call-start = ((), (), s32[]{:S(2)}) async-start(), calls=%async_computation.12 | async-start | bytes 1048576 | tf_op jit(solution)/shard_map/psum | solution.py:14
  980.4 104.9 %all-gather.15.cloned.1.call-start = ((), (), s32[]{:S(2)}) async-start(), calls=%async_computation.13 | async-start | bytes 1114112 | tf_op jit(solution)/shard_map/all_gather | solution.py:95
  1042.7 138.1 %all-reduce.33.cloned.1.call-start = ((), (), s32[]{:S(2)}) async-start(), calls=%async_computation.14 | async-start | bytes 131072 | tf_op jit(solution)/shard_map/psum | solution.py:14
  1099.5 168.3 %all-reduce.35.cloned.1.call-start = ((), (), s32[]{:S(2)}) async-start(), calls=%async_computation.15 | async-start | bytes 1048576 | tf_op jit(solution)/shard_map/psum | solution.py:14
  1205.4 106.5 %all-gather.17.cloned.1.call-start = ((), (), s32[]{:S(2)}) async-start(), calls=%async_computation.16 | async-start | bytes 1114112 | tf_op jit(solution)/shard_map/all_gather | solution.py:95
  1269.3 138.0 %all-reduce.37.cloned.1.call-start = ((), (), s32[]{:S(2)}) async-start(), calls=%async_computation.17 | async-start | bytes 131072 | tf_op jit(solution)/shard_map/psum | solution.py:14
  1325.9 166.6 %all-reduce.39.cloned.1.call-start = ((), (), s32[]{:S(2)}) async-start(), calls=%async_computation.18 | async-start | bytes 1048576 | tf_op jit(solution)/shard_map/psum | solution.py:14
  1431.8 104.8 %all-gather.19.cloned.1.call-start = ((), (), s32[]{:S(2)}) async-start(), calls=%async_computation.19 | async-start | bytes 1114112 | tf_op jit(solution)/shard_map/all_gather | solution.py:95
  1494.0 138.0 %all-reduce.41.cloned.1.call-start = ((), (), s32[]{:S(2)}) async-start(), calls=%async_computation.20 | async-start | bytes 131072 | tf_op jit(solution)/shard_map/psum | solution.py:14
  1550.7 168.1 %all-reduce.43.cloned.1.call-start = ((), (), s32[]{:S(2)}) async-start(), calls=%async_computation.21 | async-start | bytes 1048576 | tf_op jit(solution)/shard_map/psum | solution.py:14
  1656.6 106.4 %all-gather.21.cloned.1.call-start = ((), (), s32[]{:S(2)}) async-start(), calls=%async_computation.22 | async-start | bytes 1114112 | tf_op jit(solution)/shard_map/all_gather | solution.py:95
  1720.2 138.3 %all-reduce.45.cloned.1.call-start = ((), (), s32[]{:S(2)}) async-start(), calls=%async_computation.23 | async-start | bytes 131072 | tf_op jit(solution)/shard_map/psum | solution.py:14
  1763.0 183.3 %copy-start.10 = (f32[8,128,128]{2,1,0:T(8,128)S(1)}, f32[8,128,128]{2,1,0:T(8,128)}, u32[]{:S(2)}) copy-start(f32[8,128,128]{2,1,0:T(8,128)} %all-reduce.19.cloned.1.call-done) | copy-start | bytes 1572868
  1763.0 183.4 %copy-start.11 = (f32[8,128,128]{2,1,0:T(8,128)S(1)}, f32[8,128,128]{2,1,0:T(8,128)}, u32[]{:S(2)}) copy-start(f32[8,128,128]{2,1,0:T(8,128)} %all-reduce.23.cloned.1.call-done) | copy-start | bytes 1572868
  1776.5 169.9 %copy-start.13 = (f32[8,128,128]{2,1,0:T(8,128)S(1)}, f32[8,128,128]{2,1,0:T(8,128)}, u32[]{:S(2)}) copy-start(f32[8,128,128]{2,1,0:T(8,128)} %all-reduce.31.cloned.1.call-done) | copy-start | bytes 1572868
  1776.5 170.0 %copy-start.14 = (f32[8,128,128]{2,1,0:T(8,128)S(1)}, f32[8,128,128]{2,1,0:T(8,128)}, u32[]{:S(2)}) copy-start(f32[8,128,128]{2,1,0:T(8,128)} %all-reduce.35.cloned.1.call-done) | copy-start | bytes 1572868
  1776.5 170.1 %copy-start.15 = (f32[8,128,128]{2,1,0:T(8,128)S(1)}, f32[8,128,128]{2,1,0:T(8,128)}, u32[]{:S(2)}) copy-start(f32[8,128,128]{2,1,0:T(8,128)} %all-reduce.39.cloned.1.call-done) | copy-start | bytes 1572868
  1777.2 167.6 %all-reduce.47.cloned.1.call-start = ((), (), s32[]{:S(2)}) async-start(), calls=%async_computation.24 | async-start | bytes 1048576 | tf_op jit(solution)/shard_map/psum | solution.py:14
  1884.1 104.2 %all-gather.23.cloned.1.call-start = ((), (), s32[]{:S(2)}) async-start(), calls=%async_computation.25 | async-start | bytes 1114112 | tf_op jit(solution)/shard_map/all_gather | solution.py:95
  (13 other events, 269.6 us)
Sparse Core Ops, SparseCore 0:
  193.9 86.9 all-reduce.16
  307.3 58.8 all-reduce.18
  368.9 41.5 all-gather.8
  424.8 81.1 all-reduce.20
  530.7 60.6 all-reduce.22
  593.9 41.5 all-gather.10
  649.5 81.1 all-reduce.24
  755.4 60.7 all-reduce.26
  818.9 41.5 all-gather.12
  874.6 81.1 all-reduce.28
  980.5 60.6 all-reduce.30
  1043.7 41.5 all-gather.14
  1099.6 81.1 all-reduce.32
  1205.5 62.2 all-reduce.34
  1270.4 41.5 all-gather.16
  1326.0 81.2 all-reduce.36
  1432.0 60.5 all-reduce.38
  1495.1 41.5 all-gather.18
  1550.8 81.1 all-reduce.40
  1656.7 61.9 all-reduce.42
  1721.4 41.5 all-gather.20
  1777.3 81.1 all-reduce.44
  1884.2 60.5 all-reduce.46
  1946.8 41.5 all-gather.22
where the time goes:
time: 2030 us; the launch traced here: 2020 us
  waiting for transfers between devices  1560 us (77%)
  other arithmetic  214 us (11%)
  matrix products  109 us (5%)
  local copies, waits for them, and re-layouts  95.5 us (5%)
  starting transfers between devices  21.7 us (1%)
    psum x16, waiting for transfers between devices, broadcast(): return lax.psum(block, axis)  1130 us
    all_gather x8, waiting for transfers between devices, body(): cols_l = lax.all_gather(picked, 'patch', axis=0, tiled=True)  332 us
    another operation x24, other arithmetic, body(): chol = jnp.linalg.cholesky(pivot_block)  99.1 us
    all_to_all x1, waiting for transfers between devices, body(): lax.all_to_all(outgoing, ('patch', 'col'), split_axis=0, concat_axis=0, t...  97.8 us
    another operation x16, other arithmetic, body(): lax.linalg.triangular_solve(chol, stacked, left_side=True, lower=True)  83.7 us
    dot_general x8, matrix products, body(): update = jnp.einsum('rab,scb->rsac', rows_l, cols_l, precision=HIGH)  81.8 us
  transfers between devices with their start and end apart: 26, of which 25 were waited for; matrix products, arithmetic and copies ran while one was open for 2% of the time, Pallas kernels for 0%

commit v1 on v0

v1 whole, which is shorter than its diff:
```python
import functools

import jax
import jax.numpy as jnp
from jax import lax
from jax.experimental import pallas as pl
from jax.experimental.pallas import tpu as pltpu
from jax.sharding import PartitionSpec as P

K = 8
HIGH = lax.Precision.HIGHEST
F32 = jnp.float32
BF16 = jnp.bfloat16
VMEM_BYTES = 60 * 1024 * 1024
SMEM = pl.BlockSpec(memory_space=pltpu.SMEM)
WHOLE = pl.BlockSpec(memory_space=pltpu.VMEM)
NT = (((1,), (1,)), ((), ()))
TN = (((0,), (0,)), ((), ()))


def params(**more):
    return pltpu.CompilerParams(vmem_limit_bytes=VMEM_BYTES, **more)


def dot_nt(a, b):
    return lax.dot_general(a, b, NT, precision=HIGH, preferred_element_type=F32)


def eye_mask(n):
    return lax.broadcasted_iota(jnp.int32, (n, n), 0) == lax.broadcasted_iota(jnp.int32, (n, n), 1)


def pack_kernel(per, meta, x_ref, o_ref):
    first = pl.program_id(0) * per
    width = x_ref.shape[2]

    def step(t, carry):
        slot = meta[0, first + t]
        turned = meta[1, first + t]

        @pl.when((slot >= 0) & (turned == 0))
        def _():
            o_ref[t, 0:width, :] = x_ref[slot]

        @pl.when((slot >= 0) & (turned == 1))
        def _():
            o_ref[t, 0:width, :] = x_ref[slot].T

        o_ref[t, width:, :] = jnp.full((8, width), meta[2, first + t].astype(F32), F32)
        return carry

    lax.fori_loop(0, per, step, 0)


def pack(meta, contributions, ndevice, per=16):
    slots, width, _ = contributions.shape
    return pl.pallas_call(
        functools.partial(pack_kernel, per),
        grid=(ndevice // per,),
        in_specs=[SMEM, pl.BlockSpec((slots, width, width), lambda g: (0, 0, 0), pipeline_mode=pl.Buffered(1))],
        out_specs=pl.BlockSpec((per, width + 8, width), lambda g: (g, 0, 0)),
        out_shape=jax.ShapeDtypeStruct((ndevice, width + 8, width), F32),
        compiler_params=params(),
        name="pack",
    )(meta, contributions)


def place_kernel(per, last, codes, diag, x_ref, reg_ref, o_ref):
    g = pl.program_id(0)
    width = x_ref.shape[2]

    @pl.when(g == 0)
    def _():
        def clear(q, carry):
            o_ref[q] = jnp.zeros((width, width), F32)
            return carry

        lax.fori_loop(0, o_ref.shape[0], clear, 0)

    def step(t, carry):
        code = codes[g * per + t]

        @pl.when(code >= 0)
        def _():
            o_ref[code] += x_ref[t, 0:width, :]

        return carry

    lax.fori_loop(0, per, step, 0)

    @pl.when(g == last)
    def _():
        block = o_ref[diag[0]]
        o_ref[diag[0]] = 0.5 * (block + block.T) + jnp.where(eye_mask(width), reg_ref[...], 0.0)


def place(codes, diag, got, reg, per=16):
    ndevice, high, width = got.shape
    places = 128
    return pl.pallas_call(
        functools.partial(place_kernel, per, ndevice // per - 1),
        grid=(ndevice // per,),
        in_specs=[SMEM, SMEM, pl.BlockSpec((per, high, width), lambda g: (g, 0, 0)), pl.BlockSpec((1, width), lambda g: (0, 0))],
        out_specs=pl.BlockSpec((places, width, width), lambda g: (0, 0, 0), pipeline_mode=pl.Buffered(1)),
        out_shape=jax.ShapeDtypeStruct((places, width, width), F32),
        compiler_params=params(),
        name="place",
    )(codes, diag, got, reg)


def split3(a):
    one = a.astype(BF16).astype(F32)
    rest = a - one
    two = rest.astype(BF16).astype(F32)
    return one, two, rest - two


def chol_inverse(w_ref, lt_ref):
    width = w_ref.shape[0]
    sub = lax.broadcasted_iota(jnp.int32, (8, width), 0)
    lane = lax.broadcasted_iota(jnp.int32, (8, width), 1)
    for base in range(0, width, 8):
        both = w_ref[base : base + 8, :]
        rows = both[:, :width]
        unit = both[:, width:]
        cols = [jnp.broadcast_to(rows[:, base + j : base + j + 1], (8, width)) for j in range(8)]
        scale = jnp.zeros((8, width), F32)
        for j in range(8):
            root = lax.rsqrt(cols[j][j : j + 1, :])
            lower = cols[j] * root
            for i in range(j + 1, 8):
                cols[i] = cols[i] - lower * lower[i : i + 1, :]
            below = jnp.where(sub > j, lower, 0.0)
            rows = rows - below * (rows[j : j + 1, :] * root)
            unit = unit - below * (unit[j : j + 1, :] * root)
            scale = jnp.where(sub == j, root, scale)
        upper = jnp.where(lane >= sub + base, rows * scale, 0.0)
        unit = unit * scale
        lt_ref[base : base + 8, :] = upper
        w_ref[base : base + 8, width:] = unit
        if base + 8 < width:
            u1, u2, u3 = split3(upper)
            v1, v2, v3 = split3(unit)
            left = jnp.concatenate([u1, u1, u2, u2, u1, u3], 0).astype(BF16)
            w1, w2, w3 = (jnp.concatenate([a, b], 1) for a, b in ((u1, v1), (u2, v2), (u3, v3)))
            right = jnp.concatenate([w1, w2, w1, w2, w3, w1], 0).astype(BF16)
            change = lax.dot_general(left, right, TN, preferred_element_type=F32)
            w_ref[base + 8 :, :] -= change[base + 8 :, :]


def head_kernel(fill, head_ref, lh_ref, li_ref, w_ref, lt_ref):
    width = head_ref.shape[1]
    eye = jnp.where(eye_mask(width), 1.0, 0.0).astype(F32)
    n = 0
    for c in range(K):
        for r in range(K):
            at = slice(r * width, (r + 1) * width)
            if r < c:
                lh_ref[c, at, :] = jnp.zeros((width, width), F32)
                continue
            block = head_ref[n]
            n += 1
            lh_ref[c, at, :] = 0.5 * (block + block.T) if r == c else block

    def step(k, carry):
        w_ref[:, :width] = lh_ref[k, pl.ds(pl.multiple_of(k * width, width), width), :]
        w_ref[:, width:] = eye
        chol_inverse(w_ref, lt_ref)
        li_ref[k] = w_ref[:, width:]
        lh_ref[k, pl.ds(pl.multiple_of(k * width, width), width), :] = lt_ref[...].T
        for s in range(K - 1):

            @pl.when(k == s)
            def _(s=s):
                below = slice((s + 1) * width, K * width)
                solved = dot_nt(lh_ref[s, below, :], li_ref[s])
                lh_ref[s, below, :] = solved
                for j in range(s + 1, K):
                    part = solved[(j - s - 1) * width :]
                    change = dot_nt(part, part[:width])
                    for i in range(j, K):
                        at = slice(i * width, (i + 1) * width)
                        lh_ref[j, at, :] -= fill[i, j] * change[(i - j) * width : (i - j + 1) * width]

        return carry

    lax.fori_loop(0, K, step, 0)


def factor_head(fill, head):
    width = head.shape[1]
    return pl.pallas_call(
        head_kernel,
        in_specs=[SMEM, WHOLE],
        out_specs=[WHOLE, WHOLE],
        out_shape=[
            jax.ShapeDtypeStruct((K, K * width, width), F32),
            jax.ShapeDtypeStruct((K, width, width), F32),
        ],
        scratch_shapes=[pltpu.VMEM((width, 2 * width), F32), pltpu.VMEM((width, width), F32)],
        compiler_params=params(),
        name="factor_head",
    )(fill, head)


def solve_kernel(fill, which, a_ref, lh_ref, li_ref, o_ref):
    width = a_ref.shape[1]
    row = which[0]
    work = [a_ref[k] for k in range(K)]
    for k in range(K):
        solved = dot_nt(work[k], li_ref[k])
        own = lh_ref[k, k * width : (k + 1) * width, :]
        solved = jnp.where(row > k, solved, jnp.where(row == k, own, 0.0))
        o_ref[:, k * width : (k + 1) * width] = solved
        if k + 1 < K:
            change = dot_nt(solved, lh_ref[k, (k + 1) * width :, :])
            for j in range(k + 1, K):
                work[j] = work[j] - fill[0, j] * change[:, (j - k - 1) * width : (j - k) * width]


def solve(fill, which, arow, lh, li):
    width = arow.shape[1]
    return pl.pallas_call(
        solve_kernel,
        in_specs=[SMEM, SMEM, WHOLE, WHOLE, WHOLE],
        out_specs=WHOLE,
        out_shape=jax.ShapeDtypeStruct((width, K * width), F32),
        compiler_params=params(),
        name="solve",
    )(fill, which, arow, lh, li)


def schur_kernel(pair, fill, keep, a_ref, rows_ref, cols_ref, o_ref, hi_ref, lo_ref):
    g = pl.program_id(0)
    width = a_ref.shape[2]
    nrow = a_ref.shape[1] // width

    @pl.when(g == 0)
    def _():
        def split(r, carry):
            at = pl.ds(pl.multiple_of(r * width, width), width)
            rows = rows_ref[at, :]
            hi = rows.astype(BF16)
            hi_ref[at, :] = hi
            lo_ref[at, :] = (rows - hi.astype(F32)).astype(BF16)
            return carry

        lax.fori_loop(0, nrow, split, 0)

    cols = cols_ref[...].reshape(pair * width, cols_ref.shape[2])
    col_hi = cols.astype(BF16)
    col_lo = (cols - col_hi.astype(F32)).astype(BF16)

    def step(r, carry):
        at = pl.ds(pl.multiple_of(r * width, width), width)
        some = keep[r, g * pair]
        for q in range(1, pair):
            some = some + keep[r, g * pair + q]

        @pl.when(some > 0)
        def _():
            hi = hi_ref[at, :]
            product = lax.dot_general(hi, col_hi, NT, preferred_element_type=F32)
            product += lax.dot_general(hi, col_lo, NT, preferred_element_type=F32)
            product += lax.dot_general(lo_ref[at, :], col_hi, NT, preferred_element_type=F32)
            for q in range(pair):
                value = a_ref[q, at, :] - fill[r, g * pair + q] * product[:, q * width : (q + 1) * width]
                o_ref[q, at, :] = jnp.where(keep[r, g * pair + q] > 0, value, 0.0)

        @pl.when(some == 0)
        def _():
            for q in range(pair):
                o_ref[q, at, :] = jnp.zeros((width, width), F32)

        return carry

    lax.fori_loop(0, nrow, step, 0)


def trailing(fill, keep, matrix, rows_l, cols_l, pair=2):
    colslots, tall, width = matrix.shape
    depth = rows_l.shape[1]
    return pl.pallas_call(
        functools.partial(schur_kernel, pair),
        grid=(colslots // pair,),
        in_specs=[
            SMEM,
            SMEM,
            pl.BlockSpec((pair, tall, width), lambda g: (g, 0, 0)),
            pl.BlockSpec((tall, depth), lambda g: (0, 0), pipeline_mode=pl.Buffered(1)),
            pl.BlockSpec((pair, width, depth), lambda g: (g, 0, 0)),
        ],
        out_specs=pl.BlockSpec((pair, tall, width), lambda g: (g, 0, 0)),
        out_shape=jax.ShapeDtypeStruct((colslots, tall, width), F32),
        scratch_shapes=[pltpu.VMEM((tall, depth), BF16), pltpu.VMEM((tall, depth), BF16)],
        compiler_params=params(),
        name="trailing",
    )(fill, keep, matrix, rows_l, cols_l)


def route(targets, counts, pivot, rowblk, ncol, ndevice):
    slots = targets.shape[0]
    pos_first = pivot[targets[:, 0]]
    pos_second = pivot[targets[:, 1]]
    upper_pos = jnp.maximum(pos_first, pos_second)
    lower_pos = jnp.minimum(pos_first, pos_second)
    number = jnp.arange(slots, dtype=jnp.int32)
    live = number < counts[0]
    owner = upper_pos // rowblk * ncol + lower_pos % ncol
    select = (owner[:, None] == jnp.arange(ndevice, dtype=jnp.int32)[None, :]) & live[:, None]
    turned = (pos_first < pos_second).astype(jnp.int32)
    code = lower_pos // ncol * rowblk + upper_pos % rowblk
    table = jnp.stack([number, turned, code], 0)
    return jnp.max(jnp.where(select[None], table[:, :, None], -1), 1)


def body(contributions, targets, counts, pivot, fill_draw, regular):
    width = contributions.shape[1]
    npatch = lax.axis_size("patch")
    ncol = lax.axis_size("col")
    ndevice = npatch * ncol
    nblock = pivot.shape[0]
    rowblk = regular.shape[0] // width
    colslots = nblock // ncol
    patch_id = lax.axis_index("patch")
    col_id = lax.axis_index("col")

    meta = route(targets, counts, pivot, rowblk, ncol, ndevice)
    outgoing = pack(meta, contributions, ndevice)

    reg = lax.dynamic_slice_in_dim(regular, col_id * width, width, 0)
    codes = meta[2, :K]
    mine = jnp.where(patch_id == 0, jnp.eye(width, dtype=F32) * reg[None, :], 0.0)
    parts = []
    for c in range(K):
        for r in range(c, K):
            part = jnp.where(codes[c] == r, outgoing[c, :width], 0.0)
            if r == c:
                part = part + jnp.where(col_id == c, mine, 0.0)
            parts.append(part)
    head = lax.psum(jnp.stack(parts, 0), ("patch", "col"))

    got = lax.all_to_all(outgoing, ("patch", "col"), split_axis=0, concat_axis=0, tiled=True)

    drawn = fill_draw.astype(F32)
    pattern = jnp.maximum(jnp.maximum(drawn, drawn.T), jnp.eye(nblock, dtype=F32))
    lh, li = factor_head(pattern[:K, :K], head)

    diag = (patch_id * rowblk + col_id).astype(jnp.int32)[None]
    matrix = place(got[:, width, 0].astype(jnp.int32), diag, got, reg[None, :])

    arow = lax.all_to_all(matrix[:rowblk], "col", split_axis=0, concat_axis=0, tiled=True)
    row = patch_id * rowblk + col_id
    row_fill = lax.dynamic_slice(pattern, (row, 0), (1, K))
    lrow = solve(row_fill, row.astype(jnp.int32)[None], arow, lh, li)
    rows_l = lax.all_gather(lrow, "col", axis=0, tiled=True)
    cols_l = lax.all_gather(lrow, "patch", axis=0, tiled=False)

    grow = patch_id * rowblk + jnp.arange(rowblk, dtype=jnp.int32)
    gcol = jnp.arange(colslots, dtype=jnp.int32) * ncol + col_id
    keep = ((grow[:, None] >= gcol[None, :]) & (gcol >= K)[None, :]).astype(jnp.int32)
    band = lax.dynamic_slice_in_dim(pattern, patch_id * rowblk, rowblk, 0).reshape(rowblk, colslots, ncol)
    local_fill = lax.dynamic_index_in_dim(band, col_id, 2, keepdims=False)
    schur = trailing(local_fill, keep, matrix.reshape(colslots, rowblk * width, width), rows_l, cols_l)
    return (rows_l, schur.reshape(colslots, 1, rowblk * width, width))


def solution(mesh):
    in_specs = (
        P(("patch", "col"), None, None),
        P(("patch", "col"), None),
        P(("patch", "col")),
        P(),
        P(),
        P("patch"),
    )
    out_specs = (P("patch", None), P(None, "col", "patch", None))
    return jax.shard_map(body, mesh=mesh, in_specs=in_specs, out_specs=out_specs, check_vma=False)
```

time: 2030 us -> 511 us (0.25)
  waiting for transfers between devices: 1560 us -> 264 us
  other arithmetic: 214 us -> 36.8 us
  Pallas kernels: 0 us -> 131 us
  matrix products: 109 us -> 0 us
  local copies, waits for them, and re-layouts: 95.5 us -> 15.4 us
  between operations: 16.2 us -> 37.5 us
    psum x16 -> x1, waiting for transfers between devices: 1130 us -> 113 us  [body(): head = lax.psum(jnp.stack(parts, 0), ('patch', 'col'))]
    all_gather x8 -> x2, waiting for transfers between devices: 332 us -> 102 us  [the longest x1 73.1 us: body(): cols_l = lax.all_gather(lrow, 'patch', axis=0, tiled=False)]
    another operation x40 -> x2, other arithmetic: 183 us -> 0.87 us  [the longest x1 0.86 us: body(): head = lax.psum(jnp.stack(parts, 0), ('patch', 'col'))]
    pallas_call x0 -> x5, Pallas kernels: none -> 131 us  [the longest x1 58.1 us: factor_head(): pl.pallas_call(head_kernel, in_specs=[SMEM, WHOLE], out_specs=[WHOLE, WHO...]
    dot_general x10 -> x0, matrix products: 104 us -> none  [the longest x8 81.8 us: body(): update = jnp.einsum('rab,scb->rsac', rows_l, cols_l, precision=HIGH)]
    all_to_all x1, waiting for transfers between devices: 97.8 us -> 48 us  [body(): lax.all_to_all(outgoing, ('patch', 'col'), split_axis=0, concat_axis=0, t...]
    unnamed x49 -> x12, local copies, waits for them, and re-layouts: 37.3 us -> 7.08 us
    unnamed x0 -> x35, other arithmetic: none -> 29.7 us
  transfers between devices with their start and end apart: 26 -> 5, of which waited for: 25 -> 4; matrix products, arithmetic and copies ran while one was open for 2% -> 8% of each run, Pallas kernels for 0% -> 14%
where the time goes in v1:
time: 511 us; the launch traced here: 505 us
  waiting for transfers between devices  264 us (52%)
  Pallas kernels  131 us (26%)
  between operations  37.5 us (7%)
  other arithmetic  36.8 us (7%)
  starting transfers between devices  21.1 us (4%)
  local copies, waits for them, and re-layouts  15.4 us (3%)
    psum x1, waiting for transfers between devices, body(): head = lax.psum(jnp.stack(parts, 0), ('patch', 'col'))  113 us
    all_gather x1, waiting for transfers between devices, body(): cols_l = lax.all_gather(lrow, 'patch', axis=0, tiled=False)  73.1 us
    pallas_call x1, Pallas kernels, factor_head(): pl.pallas_call(head_kernel, in_specs=[SMEM, WHOLE], out_specs=[WHOLE, WHO...  58.1 us
    all_to_all x1, waiting for transfers between devices, body(): lax.all_to_all(outgoing, ('patch', 'col'), split_axis=0, concat_axis=0, t...  48 us
    pallas_call x1, Pallas kernels, trailing(): pl.pallas_call(functools.partial(schur_kernel, pair), grid=(colslots // p...  43.8 us
    unnamed x35, other arithmetic  29.7 us
    all_gather x1, waiting for transfers between devices, body(): rows_l = lax.all_gather(lrow, 'col', axis=0, tiled=True)  29.1 us
    all_to_all x1, starting transfers between devices, body(): lax.all_to_all(outgoing, ('patch', 'col'), split_axis=0, concat_axis=0, t...  11.1 us
  transfers between devices with their start and end apart: 5, of which 4 were waited for; matrix products, arithmetic and copies ran while one was open for 8% of the time, Pallas kernels for 14%

profile of v1, /device:TPU:24, one launch (start us, length us, event | category | flops | bytes accessed | tf_op | source)
XLA Modules:
  0.0 505.5 jit_solution(6505384764642656491)
XLA Ops:
  11.0 9.9 %pack.1 = f32[128,136,128]{2,1,0:T(8,128)} custom-call(s32[3,128]{1,0:T(4,128)} %select_reduce_fusion.meta, f32[64,128,128]{2,1,0:T(8,128)} %x_ref.1), custom_call_target="tpu_custom_call" | custom-call | tf_op jit(solution)/shard_map/pack/pallas_call | solution.py:57
  20.9 11.1 %all-to-all-start = ((f32[128,136,128]{2,1,0:T(8,128)}), f32[128,136,128]{2,1,0:T(8,128)}, u32[]{:S(2)}, u32[]{:S(2)}) async-start(f32[128,136,128]{2,1,0:T(8,128)} %pack.1), calls=%async_computation | async-start | bytes 17825792 | tf_op jit(solution)/shard_map/all_to_all | solution.py:343
  56.4 0.9 constant_dynamic-update-slice_fusion.35
  57.3 0.8 constant_dynamic-update-slice_fusion.34
  58.1 0.8 constant_dynamic-update-slice_fusion.33
  63.2 0.9 constant_dynamic-update-slice_fusion.27
  64.1 0.8 constant_dynamic-update-slice_fusion.26
  69.2 0.9 constant_dynamic-update-slice_fusion.20
  70.0 0.8 constant_dynamic-update-slice_fusion.19
  74.3 0.9 constant_dynamic-update-slice_fusion.14
  75.1 0.8 constant_dynamic-update-slice_fusion.13
  78.5 0.9 constant_dynamic-update-slice_fusion.9
  79.4 0.8 constant_dynamic-update-slice_fusion.8
  81.9 0.9 constant_dynamic-update-slice_fusion.5
  82.8 0.8 constant_dynamic-update-slice_fusion.4
  84.5 0.9 constant_dynamic-update-slice_fusion.2
  85.3 0.8 constant_dynamic-update-slice_fusion.1
  86.2 0.9 constant_dynamic-update-slice_fusion
  87.1 1.4 copy-done.1
  88.5 1.3 dynamic-slice_bitcast_fusion.reg_ref
  89.8 48.0 %all-to-all-done.x_ref = f32[128,136,128]{2,1,0:T(8,128)} async-done(((f32[128,136,128]{2,1,0:T(8,128)}), f32[128,136,128]{2,1,0:T(8,128)}, u32[]{:S(2)}, u32[]{:S(2)}) %all-to-all-start) | async-done | bytes 8912928 | tf_op jit(solution)/shard_map/all_to_all | solution.py:343
  137.8 3.9 fusion.1.codes
  141.7 11.0 %place.1 = f32[128,128,128]{2,1,0:T(8,128)} custom-call(s32[128]{0:T(128)} %fusion.1.codes, s32[1]{0:T(128)} %bitcast.1.diag.which, f32[128,136,128]{2,1,0:T(8,128)} %all-to-all-done.x_ref, f32[1,128]{1,0:T(1,128)} %dynamic-slice_bitcast_fusion.reg_ref), custom_call_target="tpu_custom_call" | custom-call | tf_op jit(solution)/shard_map/place/pallas_call | solution.py:100
  152.7 1.9 slice.162
  154.6 9.9 %all-to-all-start.1 = ((f32[8,128,128]{2,1,0:T(8,128)}), f32[8,128,128]{2,1,0:T(8,128)S(1)}, u32[]{:S(2)}, u32[]{:S(2)}) async-start(f32[8,128,128]{2,1,0:T(8,128)} %slice.162), calls=%async_computation.1 | async-start | bytes 1048576 | tf_op jit(solution)/shard_map/all_to_all | solution.py:352
  165.9 113.0 %all-reduce.2.cloned.1.call-done.head_ref = f32[36,128,128]{2,1,0:T(8,128)} async-done(((f32[36,128,128]{2,1,0:T(8,128)}), f32[36,128,128]{2,1,0:T(8,128)}) %all-reduce.2.cloned.1.call-update) | async-done | bytes 2359312 | tf_op jit(solution)/shard_map/psum | solution.py:341
  278.9 58.1 %factor_head.1 = (f32[8,1024,128]{2,1,0:T(8,128)}, f32[8,128,128]{2,1,0:T(8,128)}) custom-call(f32[8,8]{1,0:T(8,128)} %slice.163.fill, f32[36,128,128]{2,1,0:T(8,128)} %all-reduce.2.cloned.1.call-done.head_ref), custom_call_target="tpu_custom_call" | custom-call | tf_op jit(solution)/shard_map/factor_head/pallas_call | solution.py:192
  337.8 8.0 %solve.1 = f32[128,1024]{1,0:T(8,128)} custom-call(f32[1,8]{1,0:T(1,128)} %constant_dynamic-slice_fusion.1.fill, s32[1]{0:T(128)} %bitcast.1.diag.which, f32[8,128,128]{2,1,0:T(8,128)} %copy-done.2, f32[8,1024,128]{2,1,0:T(8,128)} %get-tuple-element.4.lh_ref, f32[8,128,128]{2,1,0:T(8,128)} %get-tuple-element.5.li_ref), custom_call_target="tpu_custom_call" | custom-call | tf_op jit(solution)/shard_map/solve/pallas_call | solution.py:223
  348.2 29.1 %all-gather.4.cloned.1.call-done.rows_ref = f32[1024,1024]{1,0:T(8,128)} async-done(((f32[128,1024]{1,0:T(8,128)}), f32[1024,1024]{1,0:T(8,128)}) %all-gather.4.cloned.1.call-update) | async-done | bytes 4194320 | tf_op jit(solution)/shard_map/all_gather | solution.py:356
  377.3 73.1 %all-gather.6.cloned.1.call-done = f32[2048,1024]{1,0:T(8,128)} async-done(((f32[128,1024]{1,0:T(8,128)}), f32[2048,1024]{1,0:T(8,128)}) %all-gather.6.cloned.1.call-update) | async-done | bytes 8388624 | tf_op jit(solution)/shard_map/all_gather | solution.py:357
  450.4 43.8 %trailing.1 = f32[16,1024,128]{2,1,0:T(8,128)} custom-call(f32[8,16]{1,0:T(8,128)} %dynamic-slice_reduce_fusion.fill, s32[8,16]{1,0:T(8,128)} %and_convert_fusion.keep, f32[16,1024,128]{2,1,0:T(8,128)} %bitcast.68, f32[1024,1024]{1,0:T(8,128)} %all-gather.4.cloned.1.call-done.rows_ref, f32[16,128,1024]{2,1,0:T(8,128)} %bitcast.69), custom_call_target="tpu_custom_call" | custom-call | tf_op jit(solution)/shard_map/trailing/pallas_call | solution.py:283
  494.2 4.8 copy.58
  (63 shorter events, 26.0 us)
Async XLA Ops:
  7.2 0.8 copy-start
  20.9 11.1 %copy-start.4 = (s32[3,128]{1,0:T(4,128)S(1)}, s32[3,128]{1,0:T(4,128)}, u32[]{:S(2)}) copy-start(s32[3,128]{1,0:T(4,128)} %select_reduce_fusion.meta) | copy-start | bytes 4612
  20.9 116.8 %all-to-all-start = ((f32[128,136,128]{2,1,0:T(8,128)}), f32[128,136,128]{2,1,0:T(8,128)}, u32[]{:S(2)}, u32[]{:S(2)}) async-start(f32[128,136,128]{2,1,0:T(8,128)} %pack.1), calls=%async_computation | async-start | bytes 17825792 | tf_op jit(solution)/shard_map/all_to_all | solution.py:343
  32.0 246.9 %all-reduce.2.cloned.1.call-start = ((), (), s32[]{:S(2)}) async-start(), calls=%async_computation.2 | async-start | bytes 4718592 | tf_op jit(solution)/shard_map/psum | solution.py:341
  87.0 1.4 copy-start.1
  141.7 22.8 %copy-start.3 = (s32[128,128]{1,0:T(8,128)S(1)}, s32[128,128]{1,0:T(8,128)}, u32[]{:S(2)}) copy-start(s32[128,128]{1,0:T(8,128)} %param.10) | copy-start | bytes 196612
  154.6 182.5 %all-to-all-start.1 = ((f32[8,128,128]{2,1,0:T(8,128)}), f32[8,128,128]{2,1,0:T(8,128)S(1)}, u32[]{:S(2)}, u32[]{:S(2)}) async-start(f32[8,128,128]{2,1,0:T(8,128)} %slice.162), calls=%async_computation.1 | async-start | bytes 1048576 | tf_op jit(solution)/shard_map/all_to_all | solution.py:352
  164.5 212.8 %all-gather.4.cloned.1.call-start = ((), (), s32[]{:S(2)}) async-start(), calls=%async_computation.3 | async-start | bytes 4718592 | tf_op jit(solution)/shard_map/all_gather | solution.py:356
  337.0 0.8 copy-start.2
  345.9 104.5 %all-gather.6.cloned.1.call-start = ((), (), s32[]{:S(2)}) async-start(), calls=%async_computation.4 | async-start | bytes 8912896 | tf_op jit(solution)/shard_map/all_gather | solution.py:357
Sparse Core Ops, SparseCore 0:
  88.6 190.2 all-reduce.1
  346.0 31.2 all-gather.3
  379.4 70.8 all-gather.5

commit v2 on v1

--- a/solution.py
+++ b/solution.py
@@ -149,17 +149,15 @@
 
 
 def head_kernel(fill, head_ref, lh_ref, li_ref, w_ref, lt_ref):
-    width = head_ref.shape[1]
+    width = head_ref.shape[2]
     eye = jnp.where(eye_mask(width), 1.0, 0.0).astype(F32)
-    n = 0
     for c in range(K):
         for r in range(K):
             at = slice(r * width, (r + 1) * width)
             if r < c:
                 lh_ref[c, at, :] = jnp.zeros((width, width), F32)
                 continue
-            block = head_ref[n]
-            n += 1
+            block = head_ref[c, r]
             lh_ref[c, at, :] = 0.5 * (block + block.T) if r == c else block
 
     def step(k, carry):
@@ -188,7 +186,7 @@
 
 
 def factor_head(fill, head):
-    width = head.shape[1]
+    width = head.shape[2]
     return pl.pallas_call(
         head_kernel,
         in_specs=[SMEM, WHOLE],
@@ -199,6 +197,7 @@
         ],
         scratch_shapes=[pltpu.VMEM((width, 2 * width), F32), pltpu.VMEM((width, width), F32)],
         compiler_params=params(),
+        cost_estimate=pl.CostEstimate(flops=60_000_000_000, bytes_accessed=16_000_000, transcendentals=0),
         name="factor_head",
     )(fill, head)
 
@@ -230,13 +229,15 @@
     )(fill, which, arow, lh, li)
 
 
-def schur_kernel(pair, fill, keep, a_ref, rows_ref, cols_ref, o_ref, hi_ref, lo_ref):
+def schur_kernel(pair, chunk, fill, keep, a_ref, rows_ref, cols_ref, o_ref, panels_ref, hi_ref, lo_ref, sem):
     g = pl.program_id(0)
     width = a_ref.shape[2]
     nrow = a_ref.shape[1] // width
 
     @pl.when(g == 0)
     def _():
+        pltpu.make_async_copy(rows_ref, panels_ref, sem).start()
+
         def split(r, carry):
             at = pl.ds(pl.multiple_of(r * width, width), width)
             rows = rows_ref[at, :]
@@ -251,37 +252,43 @@
     col_hi = cols.astype(BF16)
     col_lo = (cols - col_hi.astype(F32)).astype(BF16)
 
-    def step(r, carry):
-        at = pl.ds(pl.multiple_of(r * width, width), width)
-        some = keep[r, g * pair]
-        for q in range(1, pair):
-            some = some + keep[r, g * pair + q]
-
-        @pl.when(some > 0)
-        def _():
+    some = keep[nrow - 1, g * pair]
+    for q in range(1, pair):
+        some = some + keep[nrow - 1, g * pair + q]
+
+    @pl.when(some > 0)
+    def _():
+        def step(m, carry):
+            at = pl.ds(pl.multiple_of(m * chunk * width, chunk * width), chunk * width)
             hi = hi_ref[at, :]
             product = lax.dot_general(hi, col_hi, NT, preferred_element_type=F32)
             product += lax.dot_general(hi, col_lo, NT, preferred_element_type=F32)
             product += lax.dot_general(lo_ref[at, :], col_hi, NT, preferred_element_type=F32)
-            for q in range(pair):
-                value = a_ref[q, at, :] - fill[r, g * pair + q] * product[:, q * width : (q + 1) * width]
-                o_ref[q, at, :] = jnp.where(keep[r, g * pair + q] > 0, value, 0.0)
-
-        @pl.when(some == 0)
-        def _():
-            for q in range(pair):
-                o_ref[q, at, :] = jnp.zeros((width, width), F32)
-
-        return carry
-
-    lax.fori_loop(0, nrow, step, 0)
-
-
-def trailing(fill, keep, matrix, rows_l, cols_l, pair=2):
+            for i in range(chunk):
+                r = m * chunk + i
+                here = pl.ds(pl.multiple_of(r * width, width), width)
+                for q in range(pair):
+                    part = product[i * width : (i + 1) * width, q * width : (q + 1) * width]
+                    value = a_ref[q, here, :] - fill[r, g * pair + q] * part
+                    o_ref[q, here, :] = jnp.where(keep[r, g * pair + q] > 0, value, 0.0)
+            return carry
+
+        lax.fori_loop(0, nrow // chunk, step, 0)
+
+    @pl.when(some == 0)
+    def _():
+        o_ref[...] = jnp.zeros(o_ref.shape, F32)
+
+    @pl.when(g == pl.num_programs(0) - 1)
+    def _():
+        pltpu.make_async_copy(rows_ref, panels_ref, sem).wait()
+
+
+def trailing(fill, keep, matrix, rows_l, cols_l, pair=2, chunk=4):
     colslots, tall, width = matrix.shape
     depth = rows_l.shape[1]
     return pl.pallas_call(
-        functools.partial(schur_kernel, pair),
+        functools.partial(schur_kernel, pair, chunk),
         grid=(colslots // pair,),
         in_specs=[
             SMEM,
@@ -290,12 +297,254 @@
             pl.BlockSpec((tall, depth), lambda g: (0, 0), pipeline_mode=pl.Buffered(1)),
             pl.BlockSpec((pair, width, depth), lambda g: (g, 0, 0)),
         ],
-        out_specs=pl.BlockSpec((pair, tall, width), lambda g: (g, 0, 0)),
-        out_shape=jax.ShapeDtypeStruct((colslots, tall, width), F32),
-        scratch_shapes=[pltpu.VMEM((tall, depth), BF16), pltpu.VMEM((tall, depth), BF16)],
+        out_specs=[pl.BlockSpec((pair, tall, width), lambda g: (g, 0, 0)), pl.BlockSpec(memory_space=pl.ANY)],
+        out_shape=[
+            jax.ShapeDtypeStruct((colslots, tall, width), F32),
+            jax.ShapeDtypeStruct((tall, depth), F32),
+        ],
+        scratch_shapes=[pltpu.VMEM((tall, depth), BF16), pltpu.VMEM((tall, depth), BF16), pltpu.SemaphoreType.DMA],
         compiler_params=params(),
         name="trailing",
     )(fill, keep, matrix, rows_l, cols_l)
+
+
+RING = 4
+
+
+def turn(value, by, size=RING):
+    return lax.rem(value + (by + size), size)
+
+
+class Sends:
+    def __init__(self, ssem, rsem):
+        self.ssem, self.rsem, self.all = ssem, rsem, []
+
+    def start(self, src, dst, patch, col):
+        n = len(self.all)
+        copy = pltpu.make_async_remote_copy(
+            src_ref=src,
+            dst_ref=dst,
+            send_sem=self.ssem.at[n],
+            recv_sem=self.rsem.at[n],
+            device_id={"patch": patch, "col": col},
+            device_id_type=pl.DeviceIdType.MESH,
+        )
+        copy.start()
+        self.all.append(copy)
+        return copy
+
+    def finish(self):
+        for copy in self.all:
+            copy.wait_send()
+
+
+def meet(peers):
+    barrier = pltpu.get_barrier_semaphore()
+    for patch, col in peers:
+        pl.semaphore_signal(
+            barrier, inc=1, device_id={"patch": patch, "col": col}, device_id_type=pl.DeviceIdType.MESH
+        )
+    pl.semaphore_wait(barrier, len(peers))
+
+
+def col_ring(sends, src, items_ref, patch, col):
+    x, core = col // 2, lax.rem(col, 2)
+    there = [turn(x, by) * 2 + core for by in range(RING)]
+    other = x * 2 + (1 - core)
+    half = items_ref.shape[1] // 2
+    up = sends.start(src, items_ref.at[col], patch, there[1])
+    down = sends.start(src, items_ref.at[col], patch, there[3])
+    side = [sends.start(src, items_ref.at[col], patch, other)]
+    yield
+    up.wait_recv()
+    from_down = items_ref.at[there[3]]
+    onward = [sends.start(from_down.at[pl.ds(0, half)], from_down.at[pl.ds(0, half)], patch, there[1])]
+    side.append(sends.start(from_down, from_down, patch, other))
+    down.wait_recv()
+    from_up = items_ref.at[there[1]]
+    onward.append(sends.start(from_up.at[pl.ds(half, half)], from_up.at[pl.ds(half, half)], patch, there[3]))
+    side.append(sends.start(from_up, from_up, patch, other))
+    yield
+    for copy in onward:
+        copy.wait_recv()
+    far = items_ref.at[there[2]]
+    side.append(sends.start(far, far, patch, other))
+    yield
+    for copy in side:
+        copy.wait_recv()
+    yield
+
+
+def patch_ring(sends, src, items_ref, patch, col, swap):
+    y, z = patch // RING, lax.rem(patch, RING)
+
+    def at(first, second):
+        i, j = (first, second) if swap else (second, first)
+        return turn(y, i) * RING + turn(z, j)
+
+    size = items_ref.shape[1] // 2
+    start = size if swap else 0
+    whole = pl.ds(start, size)
+    parts = (pl.ds(start, size // 2), pl.ds(start + size // 2, size // 2))
+
+    def relay(item, rows, target):
+        return sends.start(items_ref.at[item, rows], items_ref.at[item, rows], target, col)
+
+    mine = src.at[whole]
+    up = sends.start(mine, items_ref.at[patch, whole], at(1, 0), col)
+    down = sends.start(mine, items_ref.at[patch, whole], at(3, 0), col)
+    yield
+    across = {0: [sends.start(mine, items_ref.at[patch, whole], at(0, by), col) for by in (1, 3)]}
+    yield
+    up.wait_recv()
+    onward = [relay(at(3, 0), parts[0], at(1, 0))]
+    across[3] = [relay(at(3, 0), whole, at(0, by)) for by in (1, 3)]
+    yield
+    down.wait_recv()
+    onward.append(relay(at(1, 0), parts[1], at(3, 0)))
+    across[1] = [relay(at(1, 0), whole, at(0, by)) for by in (1, 3)]
+    yield
+    for copy in onward:
+        copy.wait_recv()
+    across[2] = [relay(at(2, 0), whole, at(0, by)) for by in (1, 3)]
+    last = []
+    for i in (0, 3, 1, 2):
+        yield
+        across[i][0].wait_recv()
+        last.append(relay(at(i, 3), parts[0], at(0, 1)))
+        across[i][1].wait_recv()
+        last.append(relay(at(i, 1), parts[1], at(0, 3)))
+    yield
+    for copy in last:
+        copy.wait_recv()
+    yield
+
+
+def interleave(*steps):
+    running = list(steps)
+    while running:
+        running = [one for one in running if next(one, "end") != "end"]
+
+
+def spread_kernel(own_ref, rows_ref, cols_ref, ssem, rsem, lsem):
+    patch, col = lax.axis_index("patch"), lax.axis_index("col")
+    y, z, x, core = patch // RING, lax.rem(patch, RING), col // 2, lax.rem(col, 2)
+    meet(
+        [(turn(y, by) * RING + z, col) for by in (1, 3)]
+        + [(y * RING + turn(z, by), col) for by in (1, 3)]
+        + [(patch, turn(x, by) * 2 + core) for by in (1, 3)]
+        + [(patch, x * 2 + 1 - core)]
+    )
+    local = [
+        pltpu.make_async_copy(own_ref, rows_ref.at[col], lsem.at[0]),
+        pltpu.make_async_copy(own_ref, cols_ref.at[patch], lsem.at[1]),
+    ]
+    sends = Sends(ssem, rsem)
+    for copy in local:
+        copy.start()
+    interleave(
+        patch_ring(sends, own_ref, cols_ref, patch, col, False),
+        patch_ring(sends, own_ref, cols_ref, patch, col, True),
+        col_ring(sends, own_ref, rows_ref, patch, col),
+    )
+    sends.finish()
+    for copy in local:
+        copy.wait()
+
+
+def spread(own, npatch, ncol):
+    tall, wide = own.shape
+    copies = 48
+    return pl.pallas_call(
+        spread_kernel,
+        in_specs=[WHOLE],
+        out_specs=[pl.BlockSpec(memory_space=pl.ANY)] * 2,
+        out_shape=[
+            jax.ShapeDtypeStruct((ncol, tall, wide), F32),
+            jax.ShapeDtypeStruct((npatch, tall, wide), F32),
+        ],
+        scratch_shapes=[
+            pltpu.SemaphoreType.DMA((copies,)),
+            pltpu.SemaphoreType.DMA((copies,)),
+            pltpu.SemaphoreType.DMA((2,)),
+        ],
+        compiler_params=params(collective_id=1, has_side_effects=True),
+        name="spread",
+    )(own)
+
+
+def gather_head_kernel(npatch, x_ref, reg_ref, head_ref, got_ref, dense_ref, part_ref, piece_ref, ssem, rsem, lsem):
+    patch, col = lax.axis_index("patch"), lax.axis_index("col")
+    width = x_ref.shape[2]
+    meet(
+        [(turn(patch, by, npatch), col) for by in range(1, npatch)]
+        + [(patch, turn(col, by, K)) for by in range(1, K)]
+    )
+    sends = Sends(ssem, rsem)
+    local = pltpu.make_async_copy(x_ref.at[col], got_ref.at[col], lsem.at[0])
+    local.start()
+    first = [
+        sends.start(x_ref.at[turn(col, by, K)], got_ref.at[col], patch, turn(col, by, K)) for by in range(1, K)
+    ]
+    local.wait()
+    for copy in first:
+        copy.wait_recv()
+    reg = jnp.broadcast_to(reg_ref[...], (8, width))
+    sub = lax.broadcasted_iota(jnp.int32, (8, width), 0)
+    lane = lax.broadcasted_iota(jnp.int32, (8, width), 1)
+    codes = [got_ref[c, width:, :] for c in range(K)]
+    for r in range(K):
+        hits = [code == r for code in codes]
+        shift = jnp.where((patch == 0) & (col == r), reg, 0.0)
+        for q in range(npatch):
+            total = jnp.where(lane == sub + q * 8, shift, 0.0)
+            for c in range(K):
+                total = total + jnp.where(hits[c], got_ref[c, q * 8 : (q + 1) * 8, :], 0.0)
+            dense_ref[q, r] = total
+    second = [
+        sends.start(dense_ref.at[turn(patch, by, npatch)], part_ref.at[by - 1], turn(patch, by, npatch), col)
+        for by in range(1, npatch)
+    ]
+    total = dense_ref[patch]
+    for by, copy in enumerate(second):
+        copy.wait_recv()
+        total = total + part_ref[by]
+    piece_ref[...] = total
+    here = pl.ds(pl.multiple_of(patch * 8, 8), 8)
+    local = pltpu.make_async_copy(piece_ref, head_ref.at[col, :, here, :], lsem.at[1])
+    local.start()
+    third = [
+        sends.start(piece_ref, head_ref.at[col, :, here, :], turn(patch, by, npatch), col) for by in range(1, npatch)
+    ]
+    local.wait()
+    for copy in third:
+        copy.wait_recv()
+    interleave(col_ring(sends, head_ref.at[col], head_ref, patch, col))
+    sends.finish()
+
+
+def gather_head(outgoing, reg, npatch):
+    _, high, width = outgoing.shape
+    copies = (K - 1) + 2 * (npatch - 1) + 8
+    rows = width // npatch
+    return pl.pallas_call(
+        functools.partial(gather_head_kernel, npatch),
+        grid=(1,),
+        in_specs=[pl.BlockSpec((K, high, width), lambda g: (0, 0, 0)), pl.BlockSpec((1, width), lambda g: (0, 0))],
+        out_specs=WHOLE,
+        out_shape=jax.ShapeDtypeStruct((K, K, width, width), F32),
+        scratch_shapes=[
+            pltpu.VMEM((K, high, width), F32),
+            pltpu.VMEM((npatch, K, rows, width), F32),
+            pltpu.VMEM((npatch - 1, K, rows, width), F32),
+            pltpu.VMEM((K, rows, width), F32),
+            pltpu.SemaphoreType.DMA((copies,)),
+            pltpu.SemaphoreType.DMA((copies,)),
+            pltpu.SemaphoreType.DMA((2,)),
+        ],
+        compiler_params=params(collective_id=0, has_side_effects=True),
+        name="gather_head",
+    )(outgoing, reg)
 
 
 def route(targets, counts, pivot, rowblk, ncol, ndevice):
@@ -329,16 +578,8 @@
     outgoing = pack(meta, contributions, ndevice)
 
     reg = lax.dynamic_slice_in_dim(regular, col_id * width, width, 0)
-    codes = meta[2, :K]
-    mine = jnp.where(patch_id == 0, jnp.eye(width, dtype=F32) * reg[None, :], 0.0)
-    parts = []
-    for c in range(K):
-        for r in range(c, K):
-            part = jnp.where(codes[c] == r, outgoing[c, :width], 0.0)
-            if r == c:
-                part = part + jnp.where(col_id == c, mine, 0.0)
-            parts.append(part)
-    head = lax.psum(jnp.stack(parts, 0), ("patch", "col"))
+    head = gather_head(outgoing, reg[None, :], npatch)
+    outgoing, head = lax.optimization_barrier((outgoing, head))
 
     got = lax.all_to_all(outgoing, ("patch", "col"), split_axis=0, concat_axis=0, tiled=True)
 
@@ -353,16 +594,16 @@
     row = patch_id * rowblk + col_id
     row_fill = lax.dynamic_slice(pattern, (row, 0), (1, K))
     lrow = solve(row_fill, row.astype(jnp.int32)[None], arow, lh, li)
-    rows_l = lax.all_gather(lrow, "col", axis=0, tiled=True)
-    cols_l = lax.all_gather(lrow, "patch", axis=0, tiled=False)
+    rows_l, cols_l = spread(lrow, npatch, ncol)
+    rows_l = rows_l.reshape(rowblk * width, K * width)
 
     grow = patch_id * rowblk + jnp.arange(rowblk, dtype=jnp.int32)
     gcol = jnp.arange(colslots, dtype=jnp.int32) * ncol + col_id
     keep = ((grow[:, None] >= gcol[None, :]) & (gcol >= K)[None, :]).astype(jnp.int32)
     band = lax.dynamic_slice_in_dim(pattern, patch_id * rowblk, rowblk, 0).reshape(rowblk, colslots, ncol)
     local_fill = lax.dynamic_index_in_dim(band, col_id, 2, keepdims=False)
-    schur = trailing(local_fill, keep, matrix.reshape(colslots, rowblk * width, width), rows_l, cols_l)
-    return (rows_l, schur.reshape(colslots, 1, rowblk * width, width))
+    schur, panels = trailing(local_fill, keep, matrix.reshape(colslots, rowblk * width, width), rows_l, cols_l)
+    return (panels, schur.reshape(colslots, 1, rowblk * width, width))
 
 
 def solution(mesh):

time: 511 us -> 304 us (0.59)
  waiting for transfers between devices: 264 us -> 53.6 us
  Pallas kernels: 131 us -> 218 us
  between operations: 37.5 us -> 1.63 us
  other arithmetic: 36.8 us -> 6.19 us
  local copies, waits for them, and re-layouts: 15.4 us -> 8.4 us
  starting transfers between devices: 21.1 us -> 15.3 us
    psum x1 -> x0, waiting for transfers between devices: 113 us -> none  [body(): head = lax.psum(jnp.stack(parts, 0), ('patch', 'col'))]
    all_gather x2 -> x0, waiting for transfers between devices: 102 us -> none  [the longest x1 73.1 us: body(): cols_l = lax.all_gather(lrow, 'patch', axis=0, tiled=False)]
    pallas_call x1 -> x3, Pallas kernels: 43.8 us -> 130 us  [the longest x1 57.6 us: gather_head(): pl.pallas_call(functools.partial(gather_head_kernel, npatch), grid=(1,),...]
    unnamed x35 -> x0, other arithmetic: 29.7 us -> none
    all_to_all x1, waiting for transfers between devices: 0.01 us -> 8.21 us  [body(): lax.all_to_all(matrix[:rowblk], 'col', split_axis=0, concat_axis=0, tiled...]
    unnamed x12 -> x7, local copies, waits for them, and re-layouts: 7.08 us -> 0.9 us
  transfers between devices with their start and end apart: 5 -> 2, of which waited for: 4 -> 2; matrix products, arithmetic and copies ran while one was open for 8% -> 1% of each run, Pallas kernels for 14% -> 19%
where the time goes in v2:
time: 304 us; the launch traced here: 303 us
  Pallas kernels  218 us (72%)
  waiting for transfers between devices  53.6 us (18%)
  starting transfers between devices  15.3 us (5%)
  local copies, waits for them, and re-layouts  8.4 us (3%)
  other arithmetic  6.19 us (2%)
    pallas_call x1, Pallas kernels, factor_head(): pl.pallas_call(head_kernel, in_specs=[SMEM, WHOLE], out_specs=[WHOLE, WHO...  58.5 us
    pallas_call x1, Pallas kernels, gather_head(): pl.pallas_call(functools.partial(gather_head_kernel, npatch), grid=(1,),...  57.6 us
    pallas_call x1, Pallas kernels, spread(): pl.pallas_call(spread_kernel, in_specs=[WHOLE], out_specs=[pl.BlockSpec(m...  51.5 us
    all_to_all x1, waiting for transfers between devices, body(): lax.all_to_all(outgoing, ('patch', 'col'), split_axis=0, concat_axis=0, t...  45.4 us
    pallas_call x1, Pallas kernels, trailing(): pl.pallas_call(functools.partial(schur_kernel, pair, chunk), grid=(colslo...  20.9 us
    pallas_call x1, Pallas kernels, place(): pl.pallas_call(functools.partial(place_kernel, per, ndevice // per - 1),...  10.9 us
    pallas_call x1, Pallas kernels, pack(): pl.pallas_call(functools.partial(pack_kernel, per), grid=(ndevice // per,...  10.2 us
    all_to_all x1, waiting for transfers between devices, body(): lax.all_to_all(matrix[:rowblk], 'col', split_axis=0, concat_axis=0, tiled...  8.21 us
  transfers between devices with their start and end apart: 2, of which 2 were waited for; matrix products, arithmetic and copies ran while one was open for 1% of the time, Pallas kernels for 19%

profile of v2, /device:TPU:24, one launch (start us, length us, event | category | flops | bytes accessed | tf_op | source)
XLA Modules:
  0.0 302.8 jit_solution(6925818613480625703)
XLA Ops:
  0.6 0.0 copy-start
  0.6 0.8 fusion.9
  1.4 1.4 gather_fusion.1
  2.8 1.4 gather_fusion
  5.0 0.0 copy-done
  5.0 0.7 dynamic-slice_bitcast_fusion.reg_ref
  5.7 0.1 fusion.2
  5.8 0.7 select_reduce_fusion.meta
  6.5 10.2 %pack.1.x_ref = f32[128,136,128]{2,1,0:T(8,128)} custom-call(s32[3,128]{1,0:T(4,128)} %select_reduce_fusion.meta, f32[64,128,128]{2,1,0:T(8,128)} %x_ref.1), custom_call_target="tpu_custom_call" | custom-call | tf_op jit(solution)/shard_map/pack/pallas_call | solution.py:57
  16.6 57.6 %gather_head.1.head_ref = f32[8,8,128,128]{3,2,1,0:T(8,128)} custom-call(f32[128,136,128]{2,1,0:T(8,128)} %pack.1.x_ref, f32[1,128]{1,0:T(1,128)} %dynamic-slice_bitcast_fusion.reg_ref), custom_call_target="tpu_custom_call" | custom-call | tf_op jit(solution)/shard_map/gather_head/pallas_call | solution.py:530
  74.2 0.0 copy-start.2
  74.2 8.0 %all-to-all-start = ((f32[128,136,128]{2,1,0:T(8,128)}), f32[128,136,128]{2,1,0:T(8,128)}, u32[]{:S(2)}, u32[]{:S(2)}) async-start(f32[128,136,128]{2,1,0:T(8,128)} %pack.1.x_ref), calls=%async_computation | async-start | bytes 17825792 | tf_op jit(solution)/shard_map/all_to_all | solution.py:584
  82.2 0.0 copy-done.2
  82.2 0.1 copy.17
  82.3 0.1 copy.18
  82.5 0.6 slice.26.fill
  83.1 58.5 %factor_head.1 = (f32[8,1024,128]{2,1,0:T(8,128)}, f32[8,128,128]{2,1,0:T(8,128)}) custom-call(f32[8,8]{1,0:T(8,128)} %slice.26.fill, f32[8,8,128,128]{3,2,1,0:T(8,128)} %gather_head.1.head_ref), custom_call_target="tpu_custom_call" | custom-call | flops 60000002048 | bytes 16000000 | tf_op jit(solution)/shard_map/factor_head/pallas_call | solution.py:190
  141.6 45.4 %all-to-all-done.x_ref = f32[128,136,128]{2,1,0:T(8,128)} async-done(((f32[128,136,128]{2,1,0:T(8,128)}), f32[128,136,128]{2,1,0:T(8,128)}, u32[]{:S(2)}, u32[]{:S(2)}) %all-to-all-start) | async-done | bytes 8912928 | tf_op jit(solution)/shard_map/all_to_all | solution.py:584
  187.0 3.9 %fusion.codes = s32[128]{0:T(128)} fusion(f32[128,136,128]{2,1,0:T(8,128)} %all-to-all-done.x_ref), kind=kLoop, calls=%fused_computation.4 | loop fusion | flops 128 | bytes 1024 | tf_op jit(solution)/shard_map/convert_element_type | solution.py:591
  190.9 10.9 %place.1 = f32[128,128,128]{2,1,0:T(8,128)} custom-call(s32[128]{0:T(128)} %fusion.codes, s32[1]{0:T(128)} %bitcast.8.diag.which, f32[128,136,128]{2,1,0:T(8,128)} %all-to-all-done.x_ref, f32[1,128]{1,0:T(1,128)} %dynamic-slice_bitcast_fusion.reg_ref), custom_call_target="tpu_custom_call" | custom-call | tf_op jit(solution)/shard_map/place/pallas_call | solution.py:100
  201.8 1.9 slice.25
  203.7 7.3 %all-to-all-start.1 = ((f32[8,128,128]{2,1,0:T(8,128)}), f32[8,128,128]{2,1,0:T(8,128)S(1)}, u32[]{:S(2)}, u32[]{:S(2)}) async-start(f32[8,128,128]{2,1,0:T(8,128)} %slice.25), calls=%async_computation.1 | async-start | bytes 1048576 | tf_op jit(solution)/shard_map/all_to_all | solution.py:593
  211.0 0.1 reshape.217
  211.1 0.8 dynamic-slice_reduce_fusion.fill
  211.9 0.6 constant_dynamic-slice_fusion.fill
  212.4 0.7 and_convert_fusion.keep
  213.1 8.2 %all-to-all-done.1.a_ref = f32[8,128,128]{2,1,0:T(8,128)S(1)} async-done(((f32[8,128,128]{2,1,0:T(8,128)}), f32[8,128,128]{2,1,0:T(8,128)S(1)}, u32[]{:S(2)}, u32[]{:S(2)}) %all-to-all-start.1) | async-done | bytes 524320 | tf_op jit(solution)/shard_map/all_to_all | solution.py:593
  221.3 0.0 copy-start.1
  221.3 0.8 copy-done.1
  222.1 8.0 %solve.1.own_ref = f32[128,1024]{1,0:T(8,128)} custom-call(f32[1,8]{1,0:T(1,128)} %constant_dynamic-slice_fusion.fill, s32[1]{0:T(128)} %bitcast.8.diag.which, f32[8,128,128]{2,1,0:T(8,128)} %copy-done.1, f32[8,1024,128]{2,1,0:T(8,128)} %get-tuple-element.12.lh_ref, f32[8,128,128]{2,1,0:T(8,128)} %get-tuple-element.13.li_ref), custom_call_target="tpu_custom_call" | custom-call | tf_op jit(solution)/shard_map/solve/pallas_call | solution.py:222
  230.1 51.5 %spread.1 = (f32[8,128,1024]{2,1,0:T(8,128)}, f32[16,128,1024]{2,1,0:T(8,128)}) custom-call(f32[128,1024]{1,0:T(8,128)} %solve.1.own_ref), custom_call_target="tpu_custom_call" | custom-call | tf_op jit(solution)/shard_map/spread/pallas_call | solution.py:458
  281.7 20.9 %trailing.1 = (f32[16,1024,128]{2,1,0:T(8,128)}, f32[1024,1024]{1,0:T(8,128)}) custom-call(f32[8,16]{1,0:T(8,128)} %dynamic-slice_reduce_fusion.fill, s32[8,16]{1,0:T(8,128)} %and_convert_fusion.keep, f32[16,1024,128]{2,1,0:T(8,128)} %bitcast.32, f32[1024,1024]{1,0:T(8,128)} %bitcast.33, f32[16,128,1024]{2,1,0:T(8,128)} %get-tuple-element.15.cols_ref), custom_call_target="tpu_custom_call" | custom-call | tf_op jit(solution)/shard_map/trailing/pallas_call | solution.py:290
  (13 shorter events, 0.1 us)
Async XLA Ops:
  0.6 4.4 %copy-start = (f32[1024]{0:T(1024)S(1)}, f32[1024]{0:T(1024)}, u32[]{:S(2)}) copy-start(f32[1024]{0:T(1024)} %param.11) | copy-start | bytes 12292
  74.2 8.0 %copy-start.2 = (s32[128,128]{1,0:T(8,128)S(1)}, s32[128,128]{1,0:T(8,128)}, u32[]{:S(2)}) copy-start(s32[128,128]{1,0:T(8,128)} %param.10) | copy-start | bytes 196612
  74.2 112.8 %all-to-all-start = ((f32[128,136,128]{2,1,0:T(8,128)}), f32[128,136,128]{2,1,0:T(8,128)}, u32[]{:S(2)}, u32[]{:S(2)}) async-start(f32[128,136,128]{2,1,0:T(8,128)} %pack.1.x_ref), calls=%async_computation | async-start | bytes 17825792 | tf_op jit(solution)/shard_map/all_to_all | solution.py:584
  203.7 17.6 %all-to-all-start.1 = ((f32[8,128,128]{2,1,0:T(8,128)}), f32[8,128,128]{2,1,0:T(8,128)S(1)}, u32[]{:S(2)}, u32[]{:S(2)}) async-start(f32[8,128,128]{2,1,0:T(8,128)} %slice.25), calls=%async_computation.1 | async-start | bytes 1048576 | tf_op jit(solution)/shard_map/all_to_all | solution.py:593
  221.3 0.8 copy-start.1

commit v3 on v2

--- a/solution.py
+++ b/solution.py
@@ -1,4 +1,6 @@
 import functools
+import itertools
+import random
 
 import jax
 import jax.numpy as jnp
@@ -30,41 +32,6 @@
     return lax.broadcasted_iota(jnp.int32, (n, n), 0) == lax.broadcasted_iota(jnp.int32, (n, n), 1)
 
 
-def pack_kernel(per, meta, x_ref, o_ref):
-    first = pl.program_id(0) * per
-    width = x_ref.shape[2]
-
-    def step(t, carry):
-        slot = meta[0, first + t]
-        turned = meta[1, first + t]
-
-        @pl.when((slot >= 0) & (turned == 0))
-        def _():
-            o_ref[t, 0:width, :] = x_ref[slot]
-
-        @pl.when((slot >= 0) & (turned == 1))
-        def _():
-            o_ref[t, 0:width, :] = x_ref[slot].T
-
-        o_ref[t, width:, :] = jnp.full((8, width), meta[2, first + t].astype(F32), F32)
-        return carry
-
-    lax.fori_loop(0, per, step, 0)
-
-
-def pack(meta, contributions, ndevice, per=16):
-    slots, width, _ = contributions.shape
-    return pl.pallas_call(
-        functools.partial(pack_kernel, per),
-        grid=(ndevice // per,),
-        in_specs=[SMEM, pl.BlockSpec((slots, width, width), lambda g: (0, 0, 0), pipeline_mode=pl.Buffered(1))],
-        out_specs=pl.BlockSpec((per, width + 8, width), lambda g: (g, 0, 0)),
-        out_shape=jax.ShapeDtypeStruct((ndevice, width + 8, width), F32),
-        compiler_params=params(),
-        name="pack",
-    )(meta, contributions)
-
-
 def place_kernel(per, last, codes, diag, x_ref, reg_ref, o_ref):
     g = pl.program_id(0)
     width = x_ref.shape[2]
@@ -82,7 +49,7 @@
 
         @pl.when(code >= 0)
         def _():
-            o_ref[code] += x_ref[t, 0:width, :]
+            o_ref[code] += x_ref[t]
 
         return carry
 
@@ -95,12 +62,12 @@
 
 
 def place(codes, diag, got, reg, per=16):
-    ndevice, high, width = got.shape
+    ndevice, _, width = got.shape
     places = 128
     return pl.pallas_call(
         functools.partial(place_kernel, per, ndevice // per - 1),
         grid=(ndevice // per,),
-        in_specs=[SMEM, SMEM, pl.BlockSpec((per, high, width), lambda g: (g, 0, 0)), pl.BlockSpec((1, width), lambda g: (0, 0))],
+        in_specs=[SMEM, SMEM, pl.BlockSpec((per, width, width), lambda g: (g, 0, 0)), pl.BlockSpec((1, width), lambda g: (0, 0))],
         out_specs=pl.BlockSpec((places, width, width), lambda g: (0, 0, 0), pipeline_mode=pl.Buffered(1)),
         out_shape=jax.ShapeDtypeStruct((places, width, width), F32),
         compiler_params=params(),
@@ -148,7 +115,7 @@
             w_ref[base + 8 :, :] -= change[base + 8 :, :]
 
 
-def head_kernel(fill, head_ref, lh_ref, li_ref, w_ref, lt_ref):
+def factor_head(fill, head_ref, lh_ref, li_ref, w_ref, lt_ref):
     width = head_ref.shape[2]
     eye = jnp.where(eye_mask(width), 1.0, 0.0).astype(F32)
     for c in range(K):
@@ -183,23 +150,6 @@
         return carry
 
     lax.fori_loop(0, K, step, 0)
-
-
-def factor_head(fill, head):
-    width = head.shape[2]
-    return pl.pallas_call(
-        head_kernel,
-        in_specs=[SMEM, WHOLE],
-        out_specs=[WHOLE, WHOLE],
-        out_shape=[
-            jax.ShapeDtypeStruct((K, K * width, width), F32),
-            jax.ShapeDtypeStruct((K, width, width), F32),
-        ],
-        scratch_shapes=[pltpu.VMEM((width, 2 * width), F32), pltpu.VMEM((width, width), F32)],
-        compiler_params=params(),
-        cost_estimate=pl.CostEstimate(flops=60_000_000_000, bytes_accessed=16_000_000, transcendentals=0),
-        name="factor_head",
-    )(fill, head)
 
 
 def solve_kernel(fill, which, a_ref, lh_ref, li_ref, o_ref):
@@ -473,78 +423,212 @@
     )(own)
 
 
-def gather_head_kernel(npatch, x_ref, reg_ref, head_ref, got_ref, dense_ref, part_ref, piece_ref, ssem, rsem, lsem):
+def offsets():
+    left = [o for o in itertools.product(range(RING), range(RING), range(RING), range(2)) if any(o)]
+    random.Random(3).shuffle(left)
+
+    def links(o):
+        return [float(v in (2, want)) for v in o[:3] for want in (1, 3)]
+
+    load, order = [0.0] * 6, []
+    while left:
+        best = min(left, key=lambda o: max(map(sum, zip(load, links(o)))) - min(map(sum, zip(load, links(o)))))
+        left.remove(best)
+        order.append(best)
+        load = [sum(pair) for pair in zip(load, links(best))]
+    return order
+
+
+batches = (12, 12, 12, 12, 6, 0)
+
+
+def exchange_kernel(
+    npatch,
+    meta,
+    fill,
+    x_ref,
+    code_ref,
+    reg_ref,
+    all_ref,
+    codes_ref,
+    lh_ref,
+    li_ref,
+    out_ref,
+    mine_ref,
+    tile_ref,
+    row_ref,
+    dense_ref,
+    part_ref,
+    piece_ref,
+    head_ref,
+    w_ref,
+    lt_ref,
+    ssem,
+    rsem,
+    bulk,
+    lsem,
+):
     patch, col = lax.axis_index("patch"), lax.axis_index("col")
+    y, z, x, core = patch // RING, lax.rem(patch, RING), col // 2, lax.rem(col, 2)
+    me = patch * K + col
     width = x_ref.shape[2]
-    meet(
-        [(turn(patch, by, npatch), col) for by in range(1, npatch)]
-        + [(patch, turn(col, by, K)) for by in range(1, K)]
-    )
+    ndevice = npatch * K
+
+    sign = 1 + 2 * core
+    peers = []
+    for dy, dz, dx, dc in offsets():
+        to_patch = lax.rem(y + dy * sign, RING) * RING + lax.rem(z + dz * sign, RING)
+        to_col = lax.rem(x + dx * sign, RING) * 2 + lax.rem(core + dc, 2)
+        peers.append((to_patch, to_col))
+    barrier = pltpu.get_barrier_semaphore()
+    for to_patch, to_col in peers:
+        pl.semaphore_signal(
+            barrier, inc=1, device_id={"patch": to_patch, "col": to_col}, device_id_type=pl.DeviceIdType.MESH
+        )
+
+    def pack(d, carry):
+        block = x_ref[jnp.maximum(meta[0, d], 0)]
+        out_ref[d] = jnp.where(meta[1, d] > 0, block.T, block)
+        return carry
+
+    lax.fori_loop(0, K, pack, 0)
+    row_ref[...] = jnp.broadcast_to(code_ref[...], (8, width))
+    pl.semaphore_wait(barrier, len(peers))
+
     sends = Sends(ssem, rsem)
-    local = pltpu.make_async_copy(x_ref.at[col], got_ref.at[col], lsem.at[0])
-    local.start()
-    first = [
-        sends.start(x_ref.at[turn(col, by, K)], got_ref.at[col], patch, turn(col, by, K)) for by in range(1, K)
+
+    def flow(count):
+        for to_patch, to_col in peers[flow.done : flow.done + count]:
+            pltpu.make_async_remote_copy(
+                src_ref=out_ref.at[to_patch * K + to_col],
+                dst_ref=all_ref.at[me],
+                send_sem=bulk.at[0],
+                recv_sem=bulk.at[1],
+                device_id={"patch": to_patch, "col": to_col},
+                device_id_type=pl.DeviceIdType.MESH,
+            ).start()
+        flow.done += count
+
+    flow.done = 0
+
+    local = [
+        pltpu.make_async_copy(out_ref.at[col], mine_ref.at[col], lsem.at[0]),
+        pltpu.make_async_copy(row_ref, tile_ref.at[col], lsem.at[1]),
     ]
-    local.wait()
+    for copy in local:
+        copy.start()
+    first = []
+    for by in range(1, K):
+        to = turn(col, by, K)
+        first.append(sends.start(row_ref, tile_ref.at[col], patch, to))
+        first.append(sends.start(out_ref.at[to], mine_ref.at[col], patch, to))
+    lax.fori_loop(K, ndevice, pack, 0)
+    own = pltpu.make_async_copy(out_ref.at[me], all_ref.at[me], lsem.at[2])
+    own.start()
+    flow(4)
+    for copy in local:
+        copy.wait()
     for copy in first:
         copy.wait_recv()
     reg = jnp.broadcast_to(reg_ref[...], (8, width))
     sub = lax.broadcasted_iota(jnp.int32, (8, width), 0)
     lane = lax.broadcasted_iota(jnp.int32, (8, width), 1)
-    codes = [got_ref[c, width:, :] for c in range(K)]
+    codes = []
+    tile = jnp.zeros((8, width), F32)
+    for c in range(K):
+        row = tile_ref[c]
+        tile = jnp.where(sub == c, row, tile)
+        codes.append(jnp.broadcast_to(jnp.sum(jnp.where(lane == col, row, 0.0), 1, keepdims=True), (8, width)))
     for r in range(K):
         hits = [code == r for code in codes]
         shift = jnp.where((patch == 0) & (col == r), reg, 0.0)
         for q in range(npatch):
             total = jnp.where(lane == sub + q * 8, shift, 0.0)
             for c in range(K):
-                total = total + jnp.where(hits[c], got_ref[c, q * 8 : (q + 1) * 8, :], 0.0)
+                total = total + jnp.where(hits[c], mine_ref[c, q * 8 : (q + 1) * 8, :], 0.0)
             dense_ref[q, r] = total
-    second = [
-        sends.start(dense_ref.at[turn(patch, by, npatch)], part_ref.at[by - 1], turn(patch, by, npatch), col)
-        for by in range(1, npatch)
-    ]
+    here = pl.ds(pl.multiple_of(patch * 8, 8), 8)
+    codes_ref[here, :] = tile
+    second = []
+    tables = []
+    for by in range(1, npatch):
+        to = turn(patch, by, npatch)
+        second.append(sends.start(dense_ref.at[to], part_ref.at[by - 1], to, col))
+    for by in range(1, npatch):
+        tables.append(sends.start(codes_ref.at[here, :], codes_ref.at[here, :], turn(patch, by, npatch), col))
+    flow(batches[0])
     total = dense_ref[patch]
     for by, copy in enumerate(second):
         copy.wait_recv()
         total = total + part_ref[by]
     piece_ref[...] = total
-    here = pl.ds(pl.multiple_of(patch * 8, 8), 8)
-    local = pltpu.make_async_copy(piece_ref, head_ref.at[col, :, here, :], lsem.at[1])
+    local = pltpu.make_async_copy(piece_ref, head_ref.at[col, :, here, :], lsem.at[0])
     local.start()
     third = [
         sends.start(piece_ref, head_ref.at[col, :, here, :], turn(patch, by, npatch), col) for by in range(1, npatch)
     ]
+    flow(batches[1])
     local.wait()
     for copy in third:
         copy.wait_recv()
-    interleave(col_ring(sends, head_ref.at[col], head_ref, patch, col))
+    for count, _ in zip(batches[2:], col_ring(sends, head_ref.at[col], head_ref, patch, col)):
+        flow(count)
+    flow(len(peers) - flow.done)
+
+    factor_head(fill, head_ref, lh_ref, li_ref, w_ref, lt_ref)
+
     sends.finish()
-
-
-def gather_head(outgoing, reg, npatch):
-    _, high, width = outgoing.shape
-    copies = (K - 1) + 2 * (npatch - 1) + 8
+    for copy in tables:
+        copy.wait_recv()
+    own.wait()
+    every = pl.ds(0, ndevice - 1)
+    whole = pltpu.make_async_remote_copy(
+        src_ref=out_ref.at[every],
+        dst_ref=all_ref.at[every],
+        send_sem=bulk.at[0],
+        recv_sem=bulk.at[1],
+        device_id={"patch": peers[0][0], "col": peers[0][1]},
+        device_id_type=pl.DeviceIdType.MESH,
+    )
+    whole.wait_send()
+    whole.wait_recv()
+
+
+def exchange(meta, fill, contributions, reg, npatch):
+    slots, width, _ = contributions.shape
+    ndevice = npatch * K
+    copies = 2 * (K - 1) + 3 * (npatch - 1) + 8
     rows = width // npatch
+    block = (width, width)
     return pl.pallas_call(
-        functools.partial(gather_head_kernel, npatch),
-        grid=(1,),
-        in_specs=[pl.BlockSpec((K, high, width), lambda g: (0, 0, 0)), pl.BlockSpec((1, width), lambda g: (0, 0))],
-        out_specs=WHOLE,
-        out_shape=jax.ShapeDtypeStruct((K, K, width, width), F32),
+        functools.partial(exchange_kernel, npatch),
+        in_specs=[SMEM, SMEM, WHOLE, WHOLE, WHOLE],
+        out_specs=[pl.BlockSpec(memory_space=pl.ANY), WHOLE, WHOLE, WHOLE],
+        out_shape=[
+            jax.ShapeDtypeStruct((ndevice,) + block, F32),
+            jax.ShapeDtypeStruct((ndevice, ndevice), F32),
+            jax.ShapeDtypeStruct((K, K * width, width), F32),
+            jax.ShapeDtypeStruct((K,) + block, F32),
+        ],
         scratch_shapes=[
-            pltpu.VMEM((K, high, width), F32),
+            pltpu.VMEM((ndevice,) + block, F32),
+            pltpu.VMEM((K,) + block, F32),
+            pltpu.VMEM((K, 8, width), F32),
+            pltpu.VMEM((8, width), F32),
             pltpu.VMEM((npatch, K, rows, width), F32),
             pltpu.VMEM((npatch - 1, K, rows, width), F32),
             pltpu.VMEM((K, rows, width), F32),
+            pltpu.VMEM((K, K) + block, F32),
+            pltpu.VMEM((width, 2 * width), F32),
+            pltpu.VMEM(block, F32),
             pltpu.SemaphoreType.DMA((copies,)),
             pltpu.SemaphoreType.DMA((copies,)),
             pltpu.SemaphoreType.DMA((2,)),
+            pltpu.SemaphoreType.DMA((3,)),
         ],
         compiler_params=params(collective_id=0, has_side_effects=True),
-        name="gather_head",
-    )(outgoing, reg)
+        name="exchange",
+    )(meta[:2], fill, contributions, meta[2:].astype(F32), reg)
 
 
 def route(targets, counts, pivot, rowblk, ncol, ndevice):
@@ -575,20 +659,14 @@
     col_id = lax.axis_index("col")
 
     meta = route(targets, counts, pivot, rowblk, ncol, ndevice)
-    outgoing = pack(meta, contributions, ndevice)
-
-    reg = lax.dynamic_slice_in_dim(regular, col_id * width, width, 0)
-    head = gather_head(outgoing, reg[None, :], npatch)
-    outgoing, head = lax.optimization_barrier((outgoing, head))
-
-    got = lax.all_to_all(outgoing, ("patch", "col"), split_axis=0, concat_axis=0, tiled=True)
-
+    reg = lax.dynamic_slice_in_dim(regular, col_id * width, width, 0)[None, :]
     drawn = fill_draw.astype(F32)
     pattern = jnp.maximum(jnp.maximum(drawn, drawn.T), jnp.eye(nblock, dtype=F32))
-    lh, li = factor_head(pattern[:K, :K], head)
+    got, table, lh, li = exchange(meta, pattern[:K, :K], contributions, reg, npatch)
 
     diag = (patch_id * rowblk + col_id).astype(jnp.int32)[None]
-    matrix = place(got[:, width, 0].astype(jnp.int32), diag, got, reg[None, :])
+    codes = lax.dynamic_slice_in_dim(table, diag[0], 1, 1)[:, 0].astype(jnp.int32)
+    matrix = place(codes, diag, got, reg)
 
     arow = lax.all_to_all(matrix[:rowblk], "col", split_axis=0, concat_axis=0, tiled=True)
     row = patch_id * rowblk + col_id

time: 304 us -> 282 us (0.928)
  waiting for transfers between devices: 53.6 us -> 7.97 us
  Pallas kernels: 218 us -> 255 us
  starting transfers between devices: 15.3 us -> 3.67 us
    all_to_all x1 -> x0, waiting for transfers between devices: 45.4 us -> none  [body(): lax.all_to_all(outgoing, ('patch', 'col'), split_axis=0, concat_axis=0, t...]
    pallas_call x3 -> x1, Pallas kernels: 126 us -> 161 us  [exchange(): pl.pallas_call(functools.partial(exchange_kernel, npatch), in_specs=[SMEM...]
    all_to_all x1 -> x0, starting transfers between devices: 8 us -> none  [body(): lax.all_to_all(outgoing, ('patch', 'col'), split_axis=0, concat_axis=0, t...]
    all_to_all x1, starting transfers between devices: 7.31 us -> 3.67 us  [body(): lax.all_to_all(matrix[:rowblk], 'col', split_axis=0, concat_axis=0, tiled...]
  transfers between devices with their start and end apart: 2 -> 1, of which waited for: 2 -> 1; matrix products, arithmetic and copies ran while one was open for 1% -> 1% of each run, Pallas kernels for 19% -> 0%
where the time goes in v3:
time: 282 us; the launch traced here: 281 us
  Pallas kernels  255 us (90%)
  local copies, waits for them, and re-layouts  9.65 us (3%)
  waiting for transfers between devices  7.97 us (3%)
  other arithmetic  3.76 us (1%)
  starting transfers between devices  3.67 us (1%)
    pallas_call x1, Pallas kernels, exchange(): pl.pallas_call(functools.partial(exchange_kernel, npatch), in_specs=[SMEM...  161 us
    pallas_call x1, Pallas kernels, spread(): pl.pallas_call(spread_kernel, in_specs=[WHOLE], out_specs=[pl.BlockSpec(m...  54 us
    pallas_call x1, Pallas kernels, trailing(): pl.pallas_call(functools.partial(schur_kernel, pair, chunk), grid=(colslo...  20.9 us
    pallas_call x1, Pallas kernels, place(): pl.pallas_call(functools.partial(place_kernel, per, ndevice // per - 1),...  10.8 us
    pallas_call x1, Pallas kernels, solve(): pl.pallas_call(solve_kernel, in_specs=[SMEM, SMEM, WHOLE, WHOLE, WHOLE],...  8.01 us
    all_to_all x1, waiting for transfers between devices, body(): lax.all_to_all(matrix[:rowblk], 'col', split_axis=0, concat_axis=0, tiled...  7.97 us
  transfers between devices with their start and end apart: 1, of which 1 were waited for; matrix products, arithmetic and copies ran while one was open for 1% of the time, Pallas kernels for 0%

profile of v3, /device:TPU:24, one launch (start us, length us, event | category | flops | bytes accessed | tf_op | source)
XLA Modules:
  0.0 281.2 jit_solution(3829434787703719329)
XLA Ops:
  0.6 0.0 copy-start
  0.6 0.8 fusion.8
  1.4 1.4 gather_fusion.1
  2.8 1.4 gather_fusion
  5.0 0.1 fusion.1
  5.1 0.1 select_reduce_fusion
  5.2 0.5 slice_convert_fusion.code_ref
  5.7 0.6 slice.20.meta
  6.3 0.9 copy.17
  7.2 0.1 copy.18
  7.4 0.6 slice.28.fill
  8.0 0.0 copy-done
  8.0 0.6 dynamic-slice_bitcast_fusion.reg_ref
  8.5 160.9 %exchange.1 = (f32[128,128,128]{2,1,0:T(8,128)}, f32[128,128]{1,0:T(8,128)}, f32[8,1024,128]{2,1,0:T(8,128)}, f32[8,128,128]{2,1,0:T(8,128)}) custom-call(s32[2,128]{1,0:T(2,128)} %slice.20.meta, f32[8,8]{1,0:T(8,128)} %slice.28.fill, f32[64,128,128]{2,1,0:T(8,128)} %x_ref.1, f32[1,128]{1,0:T(1,128)} %slice_convert_fusion.code_ref, ...), custom_call_target="tpu_custom_call" | custom-call | tf_op jit(solution)/shard_map/exchange/pallas_call | solution.py:603
  169.4 1.5 convert_reduce_fusion.codes
  170.9 10.8 %place.1 = f32[128,128,128]{2,1,0:T(8,128)} custom-call(s32[128]{0:T(128)} %convert_reduce_fusion.codes, s32[1]{0:T(128)} %bitcast.8.diag.which, f32[128,128,128]{2,1,0:T(8,128)} %get-tuple-element.11.x_ref, f32[1,128]{1,0:T(1,128)} %dynamic-slice_bitcast_fusion.reg_ref), custom_call_target="tpu_custom_call" | custom-call | tf_op jit(solution)/shard_map/place/pallas_call | solution.py:67
  181.7 1.9 slice.29
  183.6 3.7 %all-to-all-start = ((f32[8,128,128]{2,1,0:T(8,128)}), f32[8,128,128]{2,1,0:T(8,128)S(1)}, u32[]{:S(2)}, u32[]{:S(2)}) async-start(f32[8,128,128]{2,1,0:T(8,128)} %slice.29), calls=%async_computation | async-start | bytes 1048576 | tf_op jit(solution)/shard_map/all_to_all | solution.py:671
  187.3 0.1 reshape.217
  187.4 0.8 dynamic-slice_reduce_fusion.fill
  188.2 0.5 constant_dynamic-slice_fusion.fill
  188.7 0.7 and_convert_fusion.keep
  189.4 8.0 %all-to-all-done.a_ref = f32[8,128,128]{2,1,0:T(8,128)S(1)} async-done(((f32[8,128,128]{2,1,0:T(8,128)}), f32[8,128,128]{2,1,0:T(8,128)S(1)}, u32[]{:S(2)}, u32[]{:S(2)}) %all-to-all-start) | async-done | bytes 524320 | tf_op jit(solution)/shard_map/all_to_all | solution.py:671
  197.3 0.0 copy-start.1
  197.3 0.8 copy-done.1
  198.1 8.0 %solve.1.own_ref = f32[128,1024]{1,0:T(8,128)} custom-call(f32[1,8]{1,0:T(1,128)} %constant_dynamic-slice_fusion.fill, s32[1]{0:T(128)} %bitcast.8.diag.which, f32[8,128,128]{2,1,0:T(8,128)} %copy-done.1, f32[8,1024,128]{2,1,0:T(8,128)} %get-tuple-element.12.lh_ref, f32[8,128,128]{2,1,0:T(8,128)} %get-tuple-element.13.li_ref), custom_call_target="tpu_custom_call" | custom-call | tf_op jit(solution)/shard_map/solve/pallas_call | solution.py:172
  206.1 54.0 %spread.1 = (f32[8,128,1024]{2,1,0:T(8,128)}, f32[16,128,1024]{2,1,0:T(8,128)}) custom-call(f32[128,1024]{1,0:T(8,128)} %solve.1.own_ref), custom_call_target="tpu_custom_call" | custom-call | tf_op jit(solution)/shard_map/spread/pallas_call | solution.py:408
  260.1 20.9 %trailing.1 = (f32[16,1024,128]{2,1,0:T(8,128)}, f32[1024,1024]{1,0:T(8,128)}) custom-call(f32[8,16]{1,0:T(8,128)} %dynamic-slice_reduce_fusion.fill, s32[8,16]{1,0:T(8,128)} %and_convert_fusion.keep, f32[16,1024,128]{2,1,0:T(8,128)} %bitcast.32, f32[1024,1024]{1,0:T(8,128)} %bitcast.33, f32[16,128,1024]{2,1,0:T(8,128)} %get-tuple-element.15.cols_ref), custom_call_target="tpu_custom_call" | custom-call | tf_op jit(solution)/shard_map/trailing/pallas_call | solution.py:240
  (13 shorter events, 0.1 us)
Async XLA Ops:
  0.6 7.3 %copy-start = (f32[1024]{0:T(1024)S(1)}, f32[1024]{0:T(1024)}, u32[]{:S(2)}) copy-start(f32[1024]{0:T(1024)} %param.11) | copy-start | bytes 12292
  183.6 13.7 %all-to-all-start = ((f32[8,128,128]{2,1,0:T(8,128)}), f32[8,128,128]{2,1,0:T(8,128)S(1)}, u32[]{:S(2)}, u32[]{:S(2)}) async-start(f32[8,128,128]{2,1,0:T(8,128)} %slice.29), calls=%async_computation | async-start | bytes 1048576 | tf_op jit(solution)/shard_map/all_to_all | solution.py:671
  197.3 0.8 copy-start.1

commit v4 on v3

--- a/solution.py
+++ b/solution.py
@@ -152,31 +152,46 @@
     lax.fori_loop(0, K, step, 0)
 
 
-def solve_kernel(fill, which, a_ref, lh_ref, li_ref, o_ref):
+def split2(a):
+    hi = a.astype(BF16)
+    return hi, (a - hi.astype(F32)).astype(BF16)
+
+
+def hand_on(lh_ref, li_ref, uh_ref, ul_ref, ih_ref, il_ref, diag_ref):
+    width = lh_ref.shape[2]
+
+    def column(k, carry):
+        diag_ref[k] = lh_ref[k, pl.ds(pl.multiple_of(k * width, width), width), :]
+        ih_ref[k], il_ref[k] = split2(li_ref[k].T)
+
+        def row(i, carry):
+            at = pl.ds(pl.multiple_of(i * width, width), width)
+            uh_ref[k, :, at], ul_ref[k, :, at] = split2(lh_ref[k, at, :].T)
+            return carry
+
+        return lax.fori_loop(k + 1, K, row, carry)
+
+    lax.fori_loop(0, K, column, 0)
+
+
+def dot3(a, b_hi, b_lo):
+    a_hi, a_lo = split2(a)
+    product = jnp.dot(a_hi, b_hi, preferred_element_type=F32)
+    product += jnp.dot(a_lo, b_hi, preferred_element_type=F32)
+    return product + jnp.dot(a_hi, b_lo, preferred_element_type=F32)
+
+
+def solve_row(row, fill, a_ref, uh_ref, ul_ref, ih_ref, il_ref, diag_ref, o_ref):
     width = a_ref.shape[1]
-    row = which[0]
     work = [a_ref[k] for k in range(K)]
     for k in range(K):
-        solved = dot_nt(work[k], li_ref[k])
-        own = lh_ref[k, k * width : (k + 1) * width, :]
-        solved = jnp.where(row > k, solved, jnp.where(row == k, own, 0.0))
+        solved = dot3(work[k], ih_ref[k], il_ref[k])
+        solved = jnp.where(row > k, solved, jnp.where(row == k, diag_ref[k], 0.0))
         o_ref[:, k * width : (k + 1) * width] = solved
         if k + 1 < K:
-            change = dot_nt(solved, lh_ref[k, (k + 1) * width :, :])
+            change = dot3(solved, uh_ref[k, :, (k + 1) * width :], ul_ref[k, :, (k + 1) * width :])
             for j in range(k + 1, K):
                 work[j] = work[j] - fill[0, j] * change[:, (j - k - 1) * width : (j - k) * width]
-
-
-def solve(fill, which, arow, lh, li):
-    width = arow.shape[1]
-    return pl.pallas_call(
-        solve_kernel,
-        in_specs=[SMEM, SMEM, WHOLE, WHOLE, WHOLE],
-        out_specs=WHOLE,
-        out_shape=jax.ShapeDtypeStruct((width, K * width), F32),
-        compiler_params=params(),
-        name="solve",
-    )(fill, which, arow, lh, li)
 
 
 def schur_kernel(pair, chunk, fill, keep, a_ref, rows_ref, cols_ref, o_ref, panels_ref, hi_ref, lo_ref, sem):
@@ -269,9 +284,10 @@
     def __init__(self, ssem, rsem):
         self.ssem, self.rsem, self.all = ssem, rsem, []
 
-    def start(self, src, dst, patch, col):
-        n = len(self.all)
-        copy = pltpu.make_async_remote_copy(
+        self.used = 0
+
+    def plan(self, n, src, dst, patch, col):
+        return pltpu.make_async_remote_copy(
             src_ref=src,
             dst_ref=dst,
             send_sem=self.ssem.at[n],
@@ -279,6 +295,10 @@
             device_id={"patch": patch, "col": col},
             device_id_type=pl.DeviceIdType.MESH,
         )
+
+    def start(self, src, dst, patch, col):
+        copy = self.plan(self.used, src, dst, patch, col)
+        self.used += 1
         copy.start()
         self.all.append(copy)
         return copy
@@ -376,20 +396,43 @@
         running = [one for one in running if next(one, "end") != "end"]
 
 
-def spread_kernel(own_ref, rows_ref, cols_ref, ssem, rsem, lsem):
+def spread_kernel(
+    fill,
+    panel_ref,
+    uh_ref,
+    ul_ref,
+    ih_ref,
+    il_ref,
+    diag_ref,
+    rows_ref,
+    cols_ref,
+    turned_ref,
+    own_ref,
+    ssem,
+    rsem,
+    lsem,
+):
     patch, col = lax.axis_index("patch"), lax.axis_index("col")
-    y, z, x, core = patch // RING, lax.rem(patch, RING), col // 2, lax.rem(col, 2)
+    y, z = patch // RING, lax.rem(patch, RING)
     meet(
-        [(turn(y, by) * RING + z, col) for by in (1, 3)]
+        [(patch, turn(col, by, K)) for by in range(1, K)]
+        + [(turn(y, by) * RING + z, col) for by in (1, 3)]
         + [(y * RING + turn(z, by), col) for by in (1, 3)]
-        + [(patch, turn(x, by) * 2 + core) for by in (1, 3)]
-        + [(patch, x * 2 + 1 - core)]
     )
+    sends = Sends(ssem, rsem)
+    local = pltpu.make_async_copy(panel_ref.at[col], turned_ref.at[col], lsem.at[0])
+    local.start()
+    first = [
+        sends.start(panel_ref.at[turn(col, by, K)], turned_ref.at[col], patch, turn(col, by, K)) for by in range(1, K)
+    ]
+    local.wait()
+    for copy in first:
+        copy.wait_recv()
+    solve_row(patch * K + col, fill, turned_ref, uh_ref, ul_ref, ih_ref, il_ref, diag_ref, own_ref)
     local = [
         pltpu.make_async_copy(own_ref, rows_ref.at[col], lsem.at[0]),
         pltpu.make_async_copy(own_ref, cols_ref.at[patch], lsem.at[1]),
     ]
-    sends = Sends(ssem, rsem)
     for copy in local:
         copy.start()
     interleave(
@@ -402,25 +445,30 @@
         copy.wait()
 
 
-def spread(own, npatch, ncol):
-    tall, wide = own.shape
-    copies = 48
+def spread(fill, matrix, factor, npatch, ncol):
+    width = matrix.shape[2]
+    block = (width, width)
+    wide = K * width
+    copies = 48 + K - 1
     return pl.pallas_call(
         spread_kernel,
-        in_specs=[WHOLE],
+        grid=(1,),
+        in_specs=[SMEM, pl.BlockSpec((K,) + block, lambda g: (0, 0, 0))] + [WHOLE] * 5,
         out_specs=[pl.BlockSpec(memory_space=pl.ANY)] * 2,
         out_shape=[
-            jax.ShapeDtypeStruct((ncol, tall, wide), F32),
-            jax.ShapeDtypeStruct((npatch, tall, wide), F32),
+            jax.ShapeDtypeStruct((ncol, width, wide), F32),
+            jax.ShapeDtypeStruct((npatch, width, wide), F32),
         ],
         scratch_shapes=[
+            pltpu.VMEM((K,) + block, F32),
+            pltpu.VMEM((width, wide), F32),
             pltpu.SemaphoreType.DMA((copies,)),
             pltpu.SemaphoreType.DMA((copies,)),
             pltpu.SemaphoreType.DMA((2,)),
         ],
         compiler_params=params(collective_id=1, has_side_effects=True),
         name="spread",
-    )(own)
+    )(fill, matrix, *factor)
 
 
 def offsets():
@@ -439,18 +487,65 @@
     return order
 
 
-batches = (12, 12, 12, 12, 6, 0)
+batches = (0, 0)
+
+
+def head_cols(sends, head_ref, patch, col, rest):
+    x, core = col // 2, lax.rem(col, 2)
+    first = sends.used
+    sends.used += 7 * RING
+
+    def copy(by, j, chip, hand, to, across):
+        ref = head_ref.at[chip * 2 + hand, pl.ds(2 * j, 2)]
+        return sends.plan(first + ((3 + by) if across else (by - 1)) * RING + j, ref, ref, patch, to)
+
+    def out(by, j):
+        return copy(by, j, x, core, turn(x, by) * 2 + core, False)
+
+    def side(by, j, hand):
+        return copy(by, j, turn(x, RING - by), hand, x * 2 + 1 - core, True)
+
+    def each(by, act):
+        for j in range(RING):
+            pl.when(j >= turn(x, RING - by))(functools.partial(act, j))
+
+    for by in (1, 3, 2):
+        each(0, lambda j: out(by, j).start())
+    each(0, lambda j: side(0, j, core).start())
+    rest()
+    for by in (1, 3, 2):
+        def pass_on(j, by=by):
+            copy(by, j, turn(x, RING - by), core, turn(x, by) * 2 + core, False).wait_recv()
+            side(by, j, core).start()
+
+        each(by, pass_on)
+    for by in range(RING):
+        each(by, lambda j: side(by, j, 1 - core).wait_recv())
+
+    def finish():
+        for by in (1, 3, 2):
+            each(0, lambda j: out(by, j).wait_send())
+        for by in range(RING):
+            each(by, lambda j: side(by, j, core).wait_send())
+
+    return finish
 
 
 def exchange_kernel(
     npatch,
-    meta,
+    slots,
+    turns,
     fill,
     x_ref,
     code_ref,
     reg_ref,
     all_ref,
     codes_ref,
+    uh_ref,
+    ul_ref,
+    ih_ref,
+    il_ref,
+    diag_ref,
     lh_ref,
     li_ref,
     out_ref,
@@ -487,8 +582,8 @@
         )
 
     def pack(d, carry):
-        block = x_ref[jnp.maximum(meta[0, d], 0)]
-        out_ref[d] = jnp.where(meta[1, d] > 0, block.T, block)
+        block = x_ref[jnp.maximum(slots[d], 0)]
+        out_ref[d] = jnp.where(turns[d] > 0, block.T, block)
         return carry
 
     lax.fori_loop(0, K, pack, 0)
@@ -525,7 +620,6 @@
     lax.fori_loop(K, ndevice, pack, 0)
     own = pltpu.make_async_copy(out_ref.at[me], all_ref.at[me], lsem.at[2])
     own.start()
-    flow(4)
     for copy in local:
         copy.wait()
     for copy in first:
@@ -571,12 +665,12 @@
     local.wait()
     for copy in third:
         copy.wait_recv()
-    for count, _ in zip(batches[2:], col_ring(sends, head_ref.at[col], head_ref, patch, col)):
-        flow(count)
-    flow(len(peers) - flow.done)
+    finish = head_cols(sends, head_ref, patch, col, lambda: flow(len(peers) - flow.done))
 
     factor_head(fill, head_ref, lh_ref, li_ref, w_ref, lt_ref)
-
+    hand_on(lh_ref, li_ref, uh_ref, ul_ref, ih_ref, il_ref, diag_ref)
+
+    finish()
     sends.finish()
     for copy in tables:
         copy.wait_recv()
@@ -594,23 +688,28 @@
     whole.wait_recv()
 
 
-def exchange(meta, fill, contributions, reg, npatch):
-    slots, width, _ = contributions.shape
+def exchange(slots, turns, codes, fill, contributions, reg, npatch):
+    width = contributions.shape[2]
     ndevice = npatch * K
-    copies = 2 * (K - 1) + 3 * (npatch - 1) + 8
+    copies = 2 * (K - 1) + 3 * (npatch - 1) + 7 * RING
     rows = width // npatch
     block = (width, width)
     return pl.pallas_call(
         functools.partial(exchange_kernel, npatch),
-        in_specs=[SMEM, SMEM, WHOLE, WHOLE, WHOLE],
-        out_specs=[pl.BlockSpec(memory_space=pl.ANY), WHOLE, WHOLE, WHOLE],
+        in_specs=[SMEM, SMEM, SMEM, WHOLE, WHOLE, WHOLE],
+        out_specs=[pl.BlockSpec(memory_space=pl.ANY)] + [WHOLE] * 6,
         out_shape=[
             jax.ShapeDtypeStruct((ndevice,) + block, F32),
             jax.ShapeDtypeStruct((ndevice, ndevice), F32),
-            jax.ShapeDtypeStruct((K, K * width, width), F32),
+            jax.ShapeDtypeStruct((K, width, K * width), BF16),
+            jax.ShapeDtypeStruct((K, width, K * width), BF16),
+            jax.ShapeDtypeStruct((K,) + block, BF16),
+            jax.ShapeDtypeStruct((K,) + block, BF16),
             jax.ShapeDtypeStruct((K,) + block, F32),
         ],
         scratch_shapes=[
+            pltpu.VMEM((K, K * width, width), F32),
+            pltpu.VMEM((K,) + block, F32),
             pltpu.VMEM((ndevice,) + block, F32),
             pltpu.VMEM((K,) + block, F32),
             pltpu.VMEM((K, 8, width), F32),
@@ -628,13 +727,14 @@
         ],
         compiler_params=params(collective_id=0, has_side_effects=True),
         name="exchange",
-    )(meta[:2], fill, contributions, meta[2:].astype(F32), reg)
+    )(slots, turns, fill, contributions, codes, reg)
 
 
 def route(targets, counts, pivot, rowblk, ncol, ndevice):
     slots = targets.shape[0]
-    pos_first = pivot[targets[:, 0]]
-    pos_second = pivot[targets[:, 1]]
+    blocks = jnp.arange(pivot.shape[0], dtype=jnp.int32)
+    position = jnp.sum(jnp.where(targets[:, :, None] == blocks, pivot, 0), 2)
+    pos_first, pos_second = position[:, 0], position[:, 1]
     upper_pos = jnp.maximum(pos_first, pos_second)
     lower_pos = jnp.minimum(pos_first, pos_second)
     number = jnp.arange(slots, dtype=jnp.int32)
@@ -643,8 +743,11 @@
     select = (owner[:, None] == jnp.arange(ndevice, dtype=jnp.int32)[None, :]) & live[:, None]
     turned = (pos_first < pos_second).astype(jnp.int32)
     code = lower_pos // ncol * rowblk + upper_pos % rowblk
-    table = jnp.stack([number, turned, code], 0)
-    return jnp.max(jnp.where(select[None], table[:, :, None], -1), 1)
+
+    def pick(value):
+        return jnp.max(jnp.where(select, value[:, None], -1), 0)
+
+    return pick(number), pick(turned), pick(code).astype(F32)[None, :]
 
 
 def body(contributions, targets, counts, pivot, fill_draw, regular):
@@ -658,21 +761,20 @@
     patch_id = lax.axis_index("patch")
     col_id = lax.axis_index("col")
 
-    meta = route(targets, counts, pivot, rowblk, ncol, ndevice)
+    slots, turns, codes = route(targets, counts, pivot, rowblk, ncol, ndevice)
     reg = lax.dynamic_slice_in_dim(regular, col_id * width, width, 0)[None, :]
+    corner = fill_draw[:K, :K]
+    corner = jnp.maximum(jnp.maximum(corner, corner.T), jnp.eye(K, dtype=jnp.int32)).astype(F32)
+    got, table, *factor = exchange(slots, turns, codes, corner, contributions, reg, npatch)
+
     drawn = fill_draw.astype(F32)
     pattern = jnp.maximum(jnp.maximum(drawn, drawn.T), jnp.eye(nblock, dtype=F32))
-    got, table, lh, li = exchange(meta, pattern[:K, :K], contributions, reg, npatch)
-
     diag = (patch_id * rowblk + col_id).astype(jnp.int32)[None]
     codes = lax.dynamic_slice_in_dim(table, diag[0], 1, 1)[:, 0].astype(jnp.int32)
     matrix = place(codes, diag, got, reg)
 
-    arow = lax.all_to_all(matrix[:rowblk], "col", split_axis=0, concat_axis=0, tiled=True)
-    row = patch_id * rowblk + col_id
-    row_fill = lax.dynamic_slice(pattern, (row, 0), (1, K))
-    lrow = solve(row_fill, row.astype(jnp.int32)[None], arow, lh, li)
-    rows_l, cols_l = spread(lrow, npatch, ncol)
+    row_fill = lax.dynamic_slice(pattern, (diag[0], 0), (1, K))
+    rows_l, cols_l = spread(row_fill, matrix, factor, npatch, ncol)
     rows_l = rows_l.reshape(rowblk * width, K * width)
 
     grow = patch_id * rowblk + jnp.arange(rowblk, dtype=jnp.int32)

time: 282 us -> 273 us (0.968)
  waiting for transfers between devices: 7.97 us -> 0 us
  Pallas kernels: 255 us -> 262 us
  local copies, waits for them, and re-layouts: 9.65 us -> 3.15 us
  starting transfers between devices: 3.67 us -> 0 us
    all_to_all x1 -> x0, waiting for transfers between devices: 7.97 us -> none  [body(): lax.all_to_all(matrix[:rowblk], 'col', split_axis=0, concat_axis=0, tiled...]
    pallas_call x2 -> x1, Pallas kernels: 62 us -> 69.4 us  [spread(): pl.pallas_call(spread_kernel, grid=(1,), in_specs=[SMEM, pl.BlockSpec((K,...]
    all_to_all x1 -> x0, starting transfers between devices: 3.67 us -> none  [body(): lax.all_to_all(matrix[:rowblk], 'col', split_axis=0, concat_axis=0, tiled...]
    slice x3 -> x2, local copies, waits for them, and re-layouts: 3.03 us -> 0.07 us  [body(): corner = fill_draw[:K, :K]]
    gather x2 -> x0, local copies, waits for them, and re-layouts: 2.86 us -> none  [the longest x1 1.43 us: route(): pos_first = pivot[targets[:, 0]]]
  transfers between devices with their start and end apart: 1 -> 0, of which waited for: 1 -> 0; matrix products, arithmetic and copies ran while one was open for 1% -> 0% of each run, Pallas kernels for 0% -> 0%
where the time goes in v4:
time: 273 us; the launch traced here: 272 us
  Pallas kernels  262 us (96%)
  other arithmetic  4.97 us (2%)
  local copies, waits for them, and re-layouts  3.15 us (1%)
    pallas_call x1, Pallas kernels, exchange(): pl.pallas_call(functools.partial(exchange_kernel, npatch), in_specs=[SMEM...  161 us
    pallas_call x1, Pallas kernels, spread(): pl.pallas_call(spread_kernel, grid=(1,), in_specs=[SMEM, pl.BlockSpec((K,...  69.4 us
    pallas_call x1, Pallas kernels, trailing(): pl.pallas_call(functools.partial(schur_kernel, pair, chunk), grid=(colslo...  20.8 us
    pallas_call x1, Pallas kernels, place(): pl.pallas_call(functools.partial(place_kernel, per, ndevice // per - 1),...  10.8 us

profile of v4, /device:TPU:24, one launch (start us, length us, event | category | flops | bytes accessed | tf_op | source)
XLA Modules:
  0.0 272.1 jit_solution(4605565202550499915)
XLA Ops:
  0.6 0.0 copy-start
  1.3 0.0 copy-done
  1.3 0.6 dynamic-slice_bitcast_fusion.reg_ref
  2.0 0.9 select_reduce_fusion
  2.9 0.7 select_reduce_fusion.1
  3.6 0.5 convert_bitcast_fusion.code_ref
  4.1 0.7 and_convert_fusion.keep
  4.8 0.9 copy.26
  5.7 0.1 copy.29
  5.8 0.6 fusion.3.fill
  6.4 0.1 copy.27
  6.5 0.6 constant_dynamic-slice_fusion.fill
  7.1 0.1 reshape.42
  7.2 0.8 dynamic-slice_reduce_fusion.fill
  8.0 161.4 %exchange.1 = (f32[128,128,128]{2,1,0:T(8,128)}, f32[128,128]{1,0:T(8,128)}, bf16[8,128,1024]{2,1,0:T(8,128)(2,1)}, bf16[8,128,1024]{2,1,0:T(8,128)(2,1)}, bf16[...) custom-call(s32[128]{0:T(128)} %get-tuple-element.34.slots, ...), custom_call_target="tpu_custom_call" | custom-call | tf_op jit(solution)/shard_map/exchange/pallas_call | solution.py:697
  169.4 1.5 convert_reduce_fusion.codes
  170.9 10.8 %place.1.panel_ref = f32[128,128,128]{2,1,0:T(8,128)} custom-call(s32[128]{0:T(128)} %convert_reduce_fusion.codes, s32[1]{0:T(128)} %bitcast.8.diag, f32[128,128,128]{2,1,0:T(8,128)} %get-tuple-element.14.x_ref, f32[1,128]{1,0:T(1,128)} %dynamic-slice_bitcast_fusion.reg_ref), custom_call_target="tpu_custom_call" | custom-call | tf_op jit(solution)/shard_map/place/pallas_call | solution.py:67
  181.8 69.4 %spread.1 = (f32[8,128,1024]{2,1,0:T(8,128)}, f32[16,128,1024]{2,1,0:T(8,128)}) custom-call(f32[1,8]{1,0:T(1,128)} %constant_dynamic-slice_fusion.fill, f32[128,128,128]{2,1,0:T(8,128)} %place.1.panel_ref, bf16[8,128,1024]{2,1,0:T(8,128)(2,1)} %get-tuple-element.15.uh_ref, bf16[8,128,1024]{2,1,0:T(8,128)(2,1)} %get-tuple-element.16.ul_ref, ...), custom_call_target="tpu_custom_call" | custom-call | tf_op jit(solution)/shard_map/spread/pallas_call | solution.py:453
  251.2 20.8 %trailing.1 = (f32[16,1024,128]{2,1,0:T(8,128)}, f32[1024,1024]{1,0:T(8,128)}) custom-call(f32[8,16]{1,0:T(8,128)} %dynamic-slice_reduce_fusion.fill, s32[8,16]{1,0:T(8,128)} %and_convert_fusion.keep, f32[16,1024,128]{2,1,0:T(8,128)} %bitcast.28, f32[1024,1024]{1,0:T(8,128)} %bitcast.29, f32[16,128,1024]{2,1,0:T(8,128)} %get-tuple-element.21.cols_ref), custom_call_target="tpu_custom_call" | custom-call | tf_op jit(solution)/shard_map/trailing/pallas_call | solution.py:255
  (11 shorter events, 0.1 us)
Async XLA Ops:
  0.6 0.7 copy-start

commit v5 on v4

--- a/solution.py
+++ b/solution.py
@@ -16,6 +16,7 @@
 VMEM_BYTES = 60 * 1024 * 1024
 SMEM = pl.BlockSpec(memory_space=pltpu.SMEM)
 WHOLE = pl.BlockSpec(memory_space=pltpu.VMEM)
+ANY = pl.BlockSpec(memory_space=pl.ANY)
 NT = (((1,), (1,)), ((), ()))
 TN = (((0,), (0,)), ((), ()))
 
@@ -30,6 +31,10 @@
 
 def eye_mask(n):
     return lax.broadcasted_iota(jnp.int32, (n, n), 0) == lax.broadcasted_iota(jnp.int32, (n, n), 1)
+
+
+def weight(drawn, i, j):
+    return jnp.where(i == j, 1, jnp.maximum(drawn[i, j], drawn[j, i])).astype(F32)
 
 
 def place_kernel(per, last, codes, diag, x_ref, reg_ref, o_ref):
@@ -145,7 +150,7 @@
                     change = dot_nt(part, part[:width])
                     for i in range(j, K):
                         at = slice(i * width, (i + 1) * width)
-                        lh_ref[j, at, :] -= fill[i, j] * change[(i - j) * width : (i - j + 1) * width]
+                        lh_ref[j, at, :] -= weight(fill, i, j) * change[(i - j) * width : (i - j + 1) * width]
 
         return carry
 
@@ -191,13 +196,15 @@
         if k + 1 < K:
             change = dot3(solved, uh_ref[k, :, (k + 1) * width :], ul_ref[k, :, (k + 1) * width :])
             for j in range(k + 1, K):
-                work[j] = work[j] - fill[0, j] * change[:, (j - k - 1) * width : (j - k) * width]
-
-
-def schur_kernel(pair, chunk, fill, keep, a_ref, rows_ref, cols_ref, o_ref, panels_ref, hi_ref, lo_ref, sem):
+                work[j] = work[j] - weight(fill, row, j) * change[:, (j - k - 1) * width : (j - k) * width]
+
+
+def schur_kernel(pair, chunk, fill, a_ref, rows_ref, cols_ref, o_ref, panels_ref, hi_ref, lo_ref, sem):
     g = pl.program_id(0)
     width = a_ref.shape[2]
     nrow = a_ref.shape[1] // width
+    grow = lax.axis_index("patch") * nrow
+    gcol = [(g * pair + q) * K + lax.axis_index("col") for q in range(pair)]
 
     @pl.when(g == 0)
     def _():
@@ -217,11 +224,9 @@
     col_hi = cols.astype(BF16)
     col_lo = (cols - col_hi.astype(F32)).astype(BF16)
 
-    some = keep[nrow - 1, g * pair]
-    for q in range(1, pair):
-        some = some + keep[nrow - 1, g * pair + q]
-
-    @pl.when(some > 0)
+    some = (grow + nrow > gcol[0]) & (gcol[pair - 1] >= K)
+
+    @pl.when(some)
     def _():
         def step(m, carry):
             at = pl.ds(pl.multiple_of(m * chunk * width, chunk * width), chunk * width)
@@ -234,13 +239,13 @@
                 here = pl.ds(pl.multiple_of(r * width, width), width)
                 for q in range(pair):
                     part = product[i * width : (i + 1) * width, q * width : (q + 1) * width]
-                    value = a_ref[q, here, :] - fill[r, g * pair + q] * part
-                    o_ref[q, here, :] = jnp.where(keep[r, g * pair + q] > 0, value, 0.0)
+                    value = a_ref[q, here, :] - weight(fill, grow + r, gcol[q]) * part
+                    o_ref[q, here, :] = jnp.where((grow + r >= gcol[q]) & (gcol[q] >= K), value, 0.0)
             return carry
 
         lax.fori_loop(0, nrow // chunk, step, 0)
 
-    @pl.when(some == 0)
+    @pl.when(jnp.logical_not(some))
     def _():
         o_ref[...] = jnp.zeros(o_ref.shape, F32)
 
@@ -249,14 +254,13 @@
         pltpu.make_async_copy(rows_ref, panels_ref, sem).wait()
 
 
-def trailing(fill, keep, matrix, rows_l, cols_l, pair=2, chunk=4):
+def trailing(fill, matrix, rows_l, cols_l, pair=2, chunk=4):
     colslots, tall, width = matrix.shape
     depth = rows_l.shape[1]
     return pl.pallas_call(
         functools.partial(schur_kernel, pair, chunk),
         grid=(colslots // pair,),
         in_specs=[
-            SMEM,
             SMEM,
             pl.BlockSpec((pair, tall, width), lambda g: (g, 0, 0)),
             pl.BlockSpec((tall, depth), lambda g: (0, 0), pipeline_mode=pl.Buffered(1)),
@@ -270,7 +274,7 @@
         scratch_shapes=[pltpu.VMEM((tall, depth), BF16), pltpu.VMEM((tall, depth), BF16), pltpu.SemaphoreType.DMA],
         compiler_params=params(),
         name="trailing",
-    )(fill, keep, matrix, rows_l, cols_l)
+    )(fill, matrix, rows_l, cols_l)
 
 
 RING = 4
@@ -399,21 +403,15 @@
 def spread_kernel(
     fill,
     panel_ref,
-    uh_ref,
-    ul_ref,
-    ih_ref,
-    il_ref,
-    diag_ref,
-    rows_ref,
-    cols_ref,
-    turned_ref,
-    own_ref,
-    ssem,
-    rsem,
-    lsem,
+    *refs,
 ):
+    stored, (rows_ref, cols_ref), held, rest = refs[:5], refs[5:7], refs[7:12], refs[12:]
+    turned_ref, own_ref, ssem, rsem, lsem = rest
     patch, col = lax.axis_index("patch"), lax.axis_index("col")
     y, z = patch // RING, lax.rem(patch, RING)
+    loads = [pltpu.make_async_copy(a, b, lsem.at[2 + n]) for n, (a, b) in enumerate(zip(stored, held))]
+    for copy in loads:
+        copy.start()
     meet(
         [(patch, turn(col, by, K)) for by in range(1, K)]
         + [(turn(y, by) * RING + z, col) for by in (1, 3)]
@@ -428,7 +426,9 @@
     local.wait()
     for copy in first:
         copy.wait_recv()
-    solve_row(patch * K + col, fill, turned_ref, uh_ref, ul_ref, ih_ref, il_ref, diag_ref, own_ref)
+    for copy in loads:
+        copy.wait()
+    solve_row(patch * K + col, fill, turned_ref, *held, own_ref)
     local = [
         pltpu.make_async_copy(own_ref, rows_ref.at[col], lsem.at[0]),
         pltpu.make_async_copy(own_ref, cols_ref.at[patch], lsem.at[1]),
@@ -453,18 +453,20 @@
     return pl.pallas_call(
         spread_kernel,
         grid=(1,),
-        in_specs=[SMEM, pl.BlockSpec((K,) + block, lambda g: (0, 0, 0))] + [WHOLE] * 5,
+        in_specs=[SMEM, pl.BlockSpec((K,) + block, lambda g: (0, 0, 0))]
+        + [pl.BlockSpec(memory_space=pl.ANY)] * 5,
         out_specs=[pl.BlockSpec(memory_space=pl.ANY)] * 2,
         out_shape=[
             jax.ShapeDtypeStruct((ncol, width, wide), F32),
             jax.ShapeDtypeStruct((npatch, width, wide), F32),
         ],
-        scratch_shapes=[
+        scratch_shapes=[pltpu.VMEM(part.shape, part.dtype) for part in factor]
+        + [
             pltpu.VMEM((K,) + block, F32),
             pltpu.VMEM((width, wide), F32),
             pltpu.SemaphoreType.DMA((copies,)),
             pltpu.SemaphoreType.DMA((copies,)),
-            pltpu.SemaphoreType.DMA((2,)),
+            pltpu.SemaphoreType.DMA((7,)),
         ],
         compiler_params=params(collective_id=1, has_side_effects=True),
         name="spread",
@@ -487,7 +489,7 @@
     return order
 
 
-batches = (0, 0)
+batches = (0, 30)
 
 
 def head_cols(sends, head_ref, patch, col, rest):
@@ -536,16 +538,32 @@
     slots,
     turns,
     fill,
-    x_ref,
+    given_ref,
     code_ref,
     reg_ref,
     all_ref,
     codes_ref,
-    uh_ref,
-    ul_ref,
-    ih_ref,
-    il_ref,
-    diag_ref,
+    *refs,
+):
+    stored, held, rest = refs[:5], refs[5:10], refs[10:]
+    exchange_steps(
+        npatch, slots, turns, fill, given_ref, code_ref, reg_ref, all_ref, codes_ref, stored, held, *rest
+    )
+
+
+def exchange_steps(
+    npatch,
+    slots,
+    turns,
+    fill,
+    given_ref,
+    code_ref,
+    reg_ref,
+    all_ref,
+    codes_ref,
+    stored,
+    held,
+    x_ref,
     lh_ref,
     li_ref,
     out_ref,
@@ -568,6 +586,8 @@
     me = patch * K + col
     width = x_ref.shape[2]
     ndevice = npatch * K
+    load = pltpu.make_async_copy(given_ref, x_ref, lsem.at[3])
+    load.start()
 
     sign = 1 + 2 * core
     peers = []
@@ -586,6 +606,7 @@
         out_ref[d] = jnp.where(turns[d] > 0, block.T, block)
         return carry
 
+    load.wait()
     lax.fori_loop(0, K, pack, 0)
     row_ref[...] = jnp.broadcast_to(code_ref[...], (8, width))
     pl.semaphore_wait(barrier, len(peers))
@@ -668,13 +689,18 @@
     finish = head_cols(sends, head_ref, patch, col, lambda: flow(len(peers) - flow.done))
 
     factor_head(fill, head_ref, lh_ref, li_ref, w_ref, lt_ref)
-    hand_on(lh_ref, li_ref, uh_ref, ul_ref, ih_ref, il_ref, diag_ref)
+    hand_on(lh_ref, li_ref, *held)
+    stores = [pltpu.make_async_copy(b, a, lsem.at[4 + n]) for n, (a, b) in enumerate(zip(stored, held))]
+    for copy in stores:
+        copy.start()
 
     finish()
     sends.finish()
     for copy in tables:
         copy.wait_recv()
     own.wait()
+    for copy in stores:
+        copy.wait()
     every = pl.ds(0, ndevice - 1)
     whole = pltpu.make_async_remote_copy(
         src_ref=out_ref.at[every],
@@ -692,22 +718,22 @@
     width = contributions.shape[2]
     ndevice = npatch * K
     copies = 2 * (K - 1) + 3 * (npatch - 1) + 7 * RING
+    wide, one = (K, width, K * width), (K, width, width)
+    factor = ((wide, BF16), (wide, BF16), (one, BF16), (one, BF16), (one, F32))
     rows = width // npatch
     block = (width, width)
     return pl.pallas_call(
         functools.partial(exchange_kernel, npatch),
-        in_specs=[SMEM, SMEM, SMEM, WHOLE, WHOLE, WHOLE],
-        out_specs=[pl.BlockSpec(memory_space=pl.ANY)] + [WHOLE] * 6,
+        in_specs=[SMEM, SMEM, SMEM, ANY, WHOLE, WHOLE],
+        out_specs=[ANY, WHOLE] + [ANY] * 5,
         out_shape=[
             jax.ShapeDtypeStruct((ndevice,) + block, F32),
             jax.ShapeDtypeStruct((ndevice, ndevice), F32),
-            jax.ShapeDtypeStruct((K, width, K * width), BF16),
-            jax.ShapeDtypeStruct((K, width, K * width), BF16),
-            jax.ShapeDtypeStruct((K,) + block, BF16),
-            jax.ShapeDtypeStruct((K,) + block, BF16),
-            jax.ShapeDtypeStruct((K,) + block, F32),
+            *(jax.ShapeDtypeStruct(shape, kind) for shape, kind in factor),
         ],
         scratch_shapes=[
+            *(pltpu.VMEM(shape, kind) for shape, kind in factor),
+            pltpu.VMEM(contributions.shape, F32),
             pltpu.VMEM((K, K * width, width), F32),
             pltpu.VMEM((K,) + block, F32),
             pltpu.VMEM((ndevice,) + block, F32),
@@ -723,7 +749,7 @@
             pltpu.SemaphoreType.DMA((copies,)),
             pltpu.SemaphoreType.DMA((copies,)),
             pltpu.SemaphoreType.DMA((2,)),
-            pltpu.SemaphoreType.DMA((3,)),
+            pltpu.SemaphoreType.DMA((9,)),
         ],
         compiler_params=params(collective_id=0, has_side_effects=True),
         name="exchange",
@@ -763,26 +789,16 @@
 
     slots, turns, codes = route(targets, counts, pivot, rowblk, ncol, ndevice)
     reg = lax.dynamic_slice_in_dim(regular, col_id * width, width, 0)[None, :]
-    corner = fill_draw[:K, :K]
-    corner = jnp.maximum(jnp.maximum(corner, corner.T), jnp.eye(K, dtype=jnp.int32)).astype(F32)
-    got, table, *factor = exchange(slots, turns, codes, corner, contributions, reg, npatch)
-
-    drawn = fill_draw.astype(F32)
-    pattern = jnp.maximum(jnp.maximum(drawn, drawn.T), jnp.eye(nblock, dtype=F32))
+    got, table, *factor = exchange(slots, turns, codes, fill_draw, contributions, reg, npatch)
+
     diag = (patch_id * rowblk + col_id).astype(jnp.int32)[None]
     codes = lax.dynamic_slice_in_dim(table, diag[0], 1, 1)[:, 0].astype(jnp.int32)
     matrix = place(codes, diag, got, reg)
 
-    row_fill = lax.dynamic_slice(pattern, (diag[0], 0), (1, K))
-    rows_l, cols_l = spread(row_fill, matrix, factor, npatch, ncol)
+    rows_l, cols_l = spread(fill_draw, matrix, factor, npatch, ncol)
     rows_l = rows_l.reshape(rowblk * width, K * width)
 
-    grow = patch_id * rowblk + jnp.arange(rowblk, dtype=jnp.int32)
-    gcol = jnp.arange(colslots, dtype=jnp.int32) * ncol + col_id
-    keep = ((grow[:, None] >= gcol[None, :]) & (gcol >= K)[None, :]).astype(jnp.int32)
-    band = lax.dynamic_slice_in_dim(pattern, patch_id * rowblk, rowblk, 0).reshape(rowblk, colslots, ncol)
-    local_fill = lax.dynamic_index_in_dim(band, col_id, 2, keepdims=False)
-    schur, panels = trailing(local_fill, keep, matrix.reshape(colslots, rowblk * width, width), rows_l, cols_l)
+    schur, panels = trailing(fill_draw, matrix.reshape(colslots, rowblk * width, width), rows_l, cols_l)
     return (panels, schur.reshape(colslots, 1, rowblk * width, width))
 
 

time: 273 us -> 261 us (0.956)
  Pallas kernels: 262 us -> 254 us
    pallas_call x1, Pallas kernels: 161 us -> 148 us  [exchange(): pl.pallas_call(functools.partial(exchange_kernel, npatch), in_specs=[SMEM...]
    pallas_call x1, Pallas kernels: 69.4 us -> 74.5 us  [spread(): pl.pallas_call(spread_kernel, grid=(1,), in_specs=[SMEM, pl.BlockSpec((K,...]
where the time goes in v5:
time: 261 us; the launch traced here: 260 us
  Pallas kernels  254 us (97%)
  other arithmetic  3.63 us (1%)
    pallas_call x1, Pallas kernels, exchange(): pl.pallas_call(functools.partial(exchange_kernel, npatch), in_specs=[SMEM...  148 us
    pallas_call x1, Pallas kernels, spread(): pl.pallas_call(spread_kernel, grid=(1,), in_specs=[SMEM, pl.BlockSpec((K,...  74.5 us
    pallas_call x1, Pallas kernels, trailing(): pl.pallas_call(functools.partial(schur_kernel, pair, chunk), grid=(colslo...  20.8 us
    pallas_call x1, Pallas kernels, place(): pl.pallas_call(functools.partial(place_kernel, per, ndevice // per - 1),...  10.8 us

profile of v5, /device:TPU:24, one launch (start us, length us, event | category | flops | bytes accessed | tf_op | source)
XLA Modules:
  0.0 260.2 jit_solution(4508029405497182248)
XLA Ops:
  0.6 0.0 copy-start
  1.3 0.0 copy-done
  1.3 0.6 dynamic-slice_bitcast_fusion.reg_ref
  1.9 0.9 select_reduce_fusion
  2.8 0.6 select_reduce_fusion.1
  3.5 0.5 convert_bitcast_fusion.code_ref
  4.0 148.4 %exchange.1 = (f32[128,128,128]{2,1,0:T(8,128)}, f32[128,128]{1,0:T(8,128)}, bf16[8,128,1024]{2,1,0:T(8,128)(2,1)}, bf16[8,128,1024]{2,1,0:T(8,128)(2,1)}, bf16[...) custom-call(s32[128]{0:T(128)} %get-tuple-element.32.slots, ...), custom_call_target="tpu_custom_call" | custom-call | tf_op jit(solution)/shard_map/exchange/pallas_call | solution.py:725
  152.4 1.5 convert_reduce_fusion.codes
  154.0 10.8 %place.1.panel_ref = f32[128,128,128]{2,1,0:T(8,128)} custom-call(s32[128]{0:T(128)} %convert_reduce_fusion.codes, s32[1]{0:T(128)} %bitcast.6.diag, f32[128,128,128]{2,1,0:T(8,128)} %get-tuple-element.14.x_ref, f32[1,128]{1,0:T(1,128)} %dynamic-slice_bitcast_fusion.reg_ref), custom_call_target="tpu_custom_call" | custom-call | tf_op jit(solution)/shard_map/place/pallas_call | solution.py:72
  164.8 74.5 %spread.1 = (f32[8,128,1024]{2,1,0:T(8,128)}, f32[16,128,1024]{2,1,0:T(8,128)}) custom-call(s32[128,128]{1,0:T(8,128)} %fill.5, f32[128,128,128]{2,1,0:T(8,128)} %place.1.panel_ref, bf16[8,128,1024]{2,1,0:T(8,128)(2,1)} %get-tuple-element.15.refs_0_, bf16[8,128,1024]{2,1,0:T(8,128)(2,1)} %get-tuple-element.16.refs_1_, ...), custom_call_target="tpu_custom_call" | custom-call | tf_op jit(solution)/shard_map/spread/pallas_call | solution.py:453
  239.3 20.8 %trailing.1 = (f32[16,1024,128]{2,1,0:T(8,128)}, f32[1024,1024]{1,0:T(8,128)}) custom-call(s32[128,128]{1,0:T(8,128)} %fill.5, f32[16,1024,128]{2,1,0:T(8,128)} %bitcast.18, f32[1024,1024]{1,0:T(8,128)} %bitcast.19, f32[16,128,1024]{2,1,0:T(8,128)} %get-tuple-element.21.cols_ref), custom_call_target="tpu_custom_call" | custom-call | tf_op jit(solution)/shard_map/trailing/pallas_call | solution.py:260
  (4 shorter events, 0.0 us)
Async XLA Ops:
  0.6 0.7 copy-start

commit v6 on v5

--- a/solution.py
+++ b/solution.py
@@ -13,7 +13,7 @@
 HIGH = lax.Precision.HIGHEST
 F32 = jnp.float32
 BF16 = jnp.bfloat16
-VMEM_BYTES = 60 * 1024 * 1024
+MIB = 1024 * 1024
 SMEM = pl.BlockSpec(memory_space=pltpu.SMEM)
 WHOLE = pl.BlockSpec(memory_space=pltpu.VMEM)
 ANY = pl.BlockSpec(memory_space=pl.ANY)
@@ -21,8 +21,8 @@
 TN = (((0,), (0,)), ((), ()))
 
 
-def params(**more):
-    return pltpu.CompilerParams(vmem_limit_bytes=VMEM_BYTES, **more)
+def params(size, **more):
+    return pltpu.CompilerParams(vmem_limit_bytes=size * MIB, **more)
 
 
 def dot_nt(a, b):
@@ -50,7 +50,7 @@
         lax.fori_loop(0, o_ref.shape[0], clear, 0)
 
     def step(t, carry):
-        code = codes[g * per + t]
+        code = codes[0, g * per + t]
 
         @pl.when(code >= 0)
         def _():
@@ -75,7 +75,7 @@
         in_specs=[SMEM, SMEM, pl.BlockSpec((per, width, width), lambda g: (g, 0, 0)), pl.BlockSpec((1, width), lambda g: (0, 0))],
         out_specs=pl.BlockSpec((places, width, width), lambda g: (0, 0, 0), pipeline_mode=pl.Buffered(1)),
         out_shape=jax.ShapeDtypeStruct((places, width, width), F32),
-        compiler_params=params(),
+        compiler_params=params(43),
         name="place",
     )(codes, diag, got, reg)
 
@@ -272,7 +272,7 @@
             jax.ShapeDtypeStruct((tall, depth), F32),
         ],
         scratch_shapes=[pltpu.VMEM((tall, depth), BF16), pltpu.VMEM((tall, depth), BF16), pltpu.SemaphoreType.DMA],
-        compiler_params=params(),
+        compiler_params=params(22),
         name="trailing",
     )(fill, matrix, rows_l, cols_l)
 
@@ -468,7 +468,7 @@
             pltpu.SemaphoreType.DMA((copies,)),
             pltpu.SemaphoreType.DMA((7,)),
         ],
-        compiler_params=params(collective_id=1, has_side_effects=True),
+        compiler_params=params(10, collective_id=1, has_side_effects=True),
         name="spread",
     )(fill, matrix, *factor)
 
@@ -542,12 +542,12 @@
     code_ref,
     reg_ref,
     all_ref,
-    codes_ref,
+    mine_codes_ref,
     *refs,
 ):
     stored, held, rest = refs[:5], refs[5:10], refs[10:]
     exchange_steps(
-        npatch, slots, turns, fill, given_ref, code_ref, reg_ref, all_ref, codes_ref, stored, held, *rest
+        npatch, slots, turns, fill, given_ref, code_ref, reg_ref, all_ref, mine_codes_ref, stored, held, *rest
     )
 
 
@@ -560,9 +560,10 @@
     code_ref,
     reg_ref,
     all_ref,
-    codes_ref,
+    mine_codes_ref,
     stored,
     held,
+    codes_ref,
     x_ref,
     lh_ref,
     li_ref,
@@ -698,6 +699,8 @@
     sends.finish()
     for copy in tables:
         copy.wait_recv()
+    lt_ref[...] = codes_ref[...].T
+    mine_codes_ref[...] = lt_ref[pl.ds(me, 1), :].astype(jnp.int32)
     own.wait()
     for copy in stores:
         copy.wait()
@@ -728,11 +731,12 @@
         out_specs=[ANY, WHOLE] + [ANY] * 5,
         out_shape=[
             jax.ShapeDtypeStruct((ndevice,) + block, F32),
-            jax.ShapeDtypeStruct((ndevice, ndevice), F32),
+            jax.ShapeDtypeStruct((1, ndevice), jnp.int32),
             *(jax.ShapeDtypeStruct(shape, kind) for shape, kind in factor),
         ],
         scratch_shapes=[
             *(pltpu.VMEM(shape, kind) for shape, kind in factor),
+            pltpu.VMEM((ndevice, ndevice), F32),
             pltpu.VMEM(contributions.shape, F32),
             pltpu.VMEM((K, K * width, width), F32),
             pltpu.VMEM((K,) + block, F32),
@@ -751,7 +755,7 @@
             pltpu.SemaphoreType.DMA((2,)),
             pltpu.SemaphoreType.DMA((9,)),
         ],
-        compiler_params=params(collective_id=0, has_side_effects=True),
+        compiler_params=params(38, collective_id=0, has_side_effects=True),
         name="exchange",
     )(slots, turns, fill, contributions, codes, reg)
 
@@ -789,11 +793,10 @@
 
     slots, turns, codes = route(targets, counts, pivot, rowblk, ncol, ndevice)
     reg = lax.dynamic_slice_in_dim(regular, col_id * width, width, 0)[None, :]
-    got, table, *factor = exchange(slots, turns, codes, fill_draw, contributions, reg, npatch)
+    got, places, *factor = exchange(slots, turns, codes, fill_draw, contributions, reg, npatch)
 
     diag = (patch_id * rowblk + col_id).astype(jnp.int32)[None]
-    codes = lax.dynamic_slice_in_dim(table, diag[0], 1, 1)[:, 0].astype(jnp.int32)
-    matrix = place(codes, diag, got, reg)
+    matrix = place(places, diag, got, reg)
 
     rows_l, cols_l = spread(fill_draw, matrix, factor, npatch, ncol)
     rows_l = rows_l.reshape(rowblk * width, K * width)

time: 261 us -> 255 us (0.977)
  Pallas kernels: 254 us -> 248 us
    pallas_call x1, Pallas kernels: 74.5 us -> 70.4 us  [spread(): pl.pallas_call(spread_kernel, grid=(1,), in_specs=[SMEM, pl.BlockSpec((K,...]
    pallas_call x1, Pallas kernels: 10.8 us -> 7.62 us  [place(): pl.pallas_call(functools.partial(place_kernel, per, ndevice // per - 1),...]
    unnamed x2 -> x8, local copies, waits for them, and re-layouts: 0.01 us -> 3.04 us
where the time goes in v6:
time: 255 us; the launch traced here: 254 us
  Pallas kernels  248 us (97%)
  local copies, waits for them, and re-layouts  3.12 us (1%)
    pallas_call x1, Pallas kernels, exchange(): pl.pallas_call(functools.partial(exchange_kernel, npatch), in_specs=[SMEM...  151 us
    pallas_call x1, Pallas kernels, spread(): pl.pallas_call(spread_kernel, grid=(1,), in_specs=[SMEM, pl.BlockSpec((K,...  70.4 us
    pallas_call x1, Pallas kernels, trailing(): pl.pallas_call(functools.partial(schur_kernel, pair, chunk), grid=(colslo...  19.5 us
    pallas_call x1, Pallas kernels, place(): pl.pallas_call(functools.partial(place_kernel, per, ndevice // per - 1),...  7.62 us

profile of v6, /device:TPU:24, one launch (start us, length us, event | category | flops | bytes accessed | tf_op | source)
XLA Modules:
  0.0 254.2 jit_solution(798174526269034643)
XLA Ops:
  0.6 0.0 copy-start
  1.3 0.0 copy-done
  1.3 0.1 dynamic-slice_bitcast_fusion.reg_ref
  1.4 0.9 select_reduce_fusion
  2.3 0.1 select_reduce_fusion.1
  2.5 0.0 copy-start.1
  2.5 2.2 copy-done.1
  4.7 0.0 copy-start.2
  4.7 0.8 copy-done.2
  5.5 151.0 %exchange.1 = (f32[128,128,128]{2,1,0:T(8,128)}, s32[1,128]{1,0:T(1,128)S(1)}, bf16[8,128,1024]{2,1,0:T(8,128)(2,1)S(1)}, bf16[8,128,1024]{2,1,0:T(8,128)(2,1)S(...) custom-call(s32[128]{0:T(128)S(1)} %get-tuple-element.30.slots, ...), custom_call_target="tpu_custom_call" | custom-call | tf_op jit(solution)/shard_map/exchange/pallas_call | solution.py:728
  156.5 0.0 copy-start.3
  156.5 7.6 %place.1.panel_ref = f32[128,128,128]{2,1,0:T(8,128)S(1)} custom-call(s32[1,128]{1,0:T(1,128)S(1)} %get-tuple-element.13.codes, s32[1]{0:T(128)} %bitcast.6.diag, f32[128,128,128]{2,1,0:T(8,128)} %get-tuple-element.14.x_ref, f32[1,128]{1,0:T(1,128)S(1)} %dynamic-slice_bitcast_fusion.reg_ref), custom_call_target="tpu_custom_call" | custom-call | tf_op jit(solution)/shard_map/place/pallas_call | solution.py:72
  164.1 0.0 copy-done.3
  164.2 70.4 %spread.1 = (f32[8,128,1024]{2,1,0:T(8,128)S(1)}, f32[16,128,1024]{2,1,0:T(8,128)S(1)}) custom-call(s32[128,128]{1,0:T(8,128)S(1)} %copy-done.3, f32[128,128,128]{2,1,0:T(8,128)S(1)} %place.1.panel_ref, bf16[8,128,1024]{2,1,0:T(8,128)(2,1)S(1)} %get-tuple-element.15.refs_0_, bf16[8,128,1024]{2,1,0:T(8,128)(2,1)S(1)} %get-tuple-element.16.refs_1_, ...), custom_call_target="tpu_custom_call" | custom-call | tf_op jit(solution)/shard_map/spread/pallas_call | solution.py:453
  234.5 19.5 %trailing.1 = (f32[16,1024,128]{2,1,0:T(8,128)}, f32[1024,1024]{1,0:T(8,128)}) custom-call(s32[128,128]{1,0:T(8,128)S(1)} %copy-done.3, f32[16,1024,128]{2,1,0:T(8,128)S(1)} %bitcast.18, f32[1024,1024]{1,0:T(8,128)S(1)} %bitcast.19, f32[16,128,1024]{2,1,0:T(8,128)S(1)} %get-tuple-element.21.cols_ref), custom_call_target="tpu_custom_call" | custom-call | tf_op jit(solution)/shard_map/trailing/pallas_call | solution.py:260
  (5 shorter events, 0.0 us)
Async XLA Ops:
  0.6 0.7 copy-start
  2.5 2.2 copy-start.1
  4.7 0.8 copy-start.2
  156.5 7.6 %copy-start.3 = (s32[128,128]{1,0:T(8,128)S(1)}, s32[128,128]{1,0:T(8,128)}, u32[]{:S(2)}) copy-start(s32[128,128]{1,0:T(8,128)} %fill.5) | copy-start | bytes 196612

commit v7 on v6

--- a/solution.py
+++ b/solution.py
@@ -17,6 +17,7 @@
 SMEM = pl.BlockSpec(memory_space=pltpu.SMEM)
 WHOLE = pl.BlockSpec(memory_space=pltpu.VMEM)
 ANY = pl.BlockSpec(memory_space=pl.ANY)
+HBM = pl.BlockSpec(memory_space=pltpu.HBM)
 NT = (((1,), (1,)), ((), ()))
 TN = (((0,), (0,)), ((), ()))
 
@@ -401,15 +402,16 @@
 
 
 def spread_kernel(
-    fill,
+    drawn_ref,
     panel_ref,
     *refs,
 ):
     stored, (rows_ref, cols_ref), held, rest = refs[:5], refs[5:7], refs[7:12], refs[12:]
-    turned_ref, own_ref, ssem, rsem, lsem = rest
+    turned_ref, own_ref, fill, ssem, rsem, lsem = rest
     patch, col = lax.axis_index("patch"), lax.axis_index("col")
     y, z = patch // RING, lax.rem(patch, RING)
     loads = [pltpu.make_async_copy(a, b, lsem.at[2 + n]) for n, (a, b) in enumerate(zip(stored, held))]
+    loads.append(pltpu.make_async_copy(drawn_ref, fill, lsem.at[7]))
     for copy in loads:
         copy.start()
     meet(
@@ -453,7 +455,7 @@
     return pl.pallas_call(
         spread_kernel,
         grid=(1,),
-        in_specs=[SMEM, pl.BlockSpec((K,) + block, lambda g: (0, 0, 0))]
+        in_specs=[HBM, pl.BlockSpec((K,) + block, lambda g: (0, 0, 0))]
         + [pl.BlockSpec(memory_space=pl.ANY)] * 5,
         out_specs=[pl.BlockSpec(memory_space=pl.ANY)] * 2,
         out_shape=[
@@ -464,9 +466,10 @@
         + [
             pltpu.VMEM((K,) + block, F32),
             pltpu.VMEM((width, wide), F32),
+            pltpu.SMEM(fill.shape, jnp.int32),
             pltpu.SemaphoreType.DMA((copies,)),
             pltpu.SemaphoreType.DMA((copies,)),
-            pltpu.SemaphoreType.DMA((7,)),
+            pltpu.SemaphoreType.DMA((8,)),
         ],
         compiler_params=params(10, collective_id=1, has_side_effects=True),
         name="spread",
@@ -480,16 +483,21 @@
     def links(o):
         return [float(v in (2, want)) for v in o[:3] for want in (1, 3)]
 
-    load, order = [0.0] * 6, []
-    while left:
-        best = min(left, key=lambda o: max(map(sum, zip(load, links(o)))) - min(map(sum, zip(load, links(o)))))
-        left.remove(best)
-        order.append(best)
-        load = [sum(pair) for pair in zip(load, links(best))]
+    def hops(o):
+        return sum(min(v, RING - v) for v in o[:2])
+
+    order = []
+    for group in ([o for o in left if hops(o) <= 1], [o for o in left if hops(o) > 1]):
+        load = [0.0] * 6
+        while group:
+            best = min(group, key=lambda o: max(map(sum, zip(load, links(o)))) - min(map(sum, zip(load, links(o)))))
+            group.remove(best)
+            order.append(best)
+            load = [sum(pair) for pair in zip(load, links(best))]
     return order
 
 
-batches = (0, 30)
+batches = (30, 20)
 
 
 def head_cols(sends, head_ref, patch, col, rest):
@@ -555,7 +563,7 @@
     npatch,
     slots,
     turns,
-    fill,
+    drawn_ref,
     given_ref,
     code_ref,
     reg_ref,
@@ -564,6 +572,7 @@
     stored,
     held,
     codes_ref,
+    fill,
     x_ref,
     lh_ref,
     li_ref,
@@ -589,6 +598,8 @@
     ndevice = npatch * K
     load = pltpu.make_async_copy(given_ref, x_ref, lsem.at[3])
     load.start()
+    draw = pltpu.make_async_copy(drawn_ref, fill, lsem.at[9])
+    draw.start()
 
     sign = 1 + 2 * core
     peers = []
@@ -689,6 +700,7 @@
         copy.wait_recv()
     finish = head_cols(sends, head_ref, patch, col, lambda: flow(len(peers) - flow.done))
 
+    draw.wait()
     factor_head(fill, head_ref, lh_ref, li_ref, w_ref, lt_ref)
     hand_on(lh_ref, li_ref, *held)
     stores = [pltpu.make_async_copy(b, a, lsem.at[4 + n]) for n, (a, b) in enumerate(zip(stored, held))]
@@ -727,7 +739,7 @@
     block = (width, width)
     return pl.pallas_call(
         functools.partial(exchange_kernel, npatch),
-        in_specs=[SMEM, SMEM, SMEM, ANY, WHOLE, WHOLE],
+        in_specs=[SMEM, SMEM, HBM, HBM, WHOLE, WHOLE],
         out_specs=[ANY, WHOLE] + [ANY] * 5,
         out_shape=[
             jax.ShapeDtypeStruct((ndevice,) + block, F32),
@@ -737,6 +749,7 @@
         scratch_shapes=[
             *(pltpu.VMEM(shape, kind) for shape, kind in factor),
             pltpu.VMEM((ndevice, ndevice), F32),
+            pltpu.SMEM(fill.shape, jnp.int32),
             pltpu.VMEM(contributions.shape, F32),
             pltpu.VMEM((K, K * width, width), F32),
             pltpu.VMEM((K,) + block, F32),
@@ -753,9 +766,9 @@
             pltpu.SemaphoreType.DMA((copies,)),
             pltpu.SemaphoreType.DMA((copies,)),
             pltpu.SemaphoreType.DMA((2,)),
-            pltpu.SemaphoreType.DMA((9,)),
+            pltpu.SemaphoreType.DMA((10,)),
         ],
-        compiler_params=params(38, collective_id=0, has_side_effects=True),
+        compiler_params=params(46, collective_id=0, has_side_effects=True),
         name="exchange",
     )(slots, turns, fill, contributions, codes, reg)
 
@@ -791,14 +804,15 @@
     patch_id = lax.axis_index("patch")
     col_id = lax.axis_index("col")
 
+    still = pltpu.with_memory_space_constraint(fill_draw, pltpu.HBM)
     slots, turns, codes = route(targets, counts, pivot, rowblk, ncol, ndevice)
     reg = lax.dynamic_slice_in_dim(regular, col_id * width, width, 0)[None, :]
-    got, places, *factor = exchange(slots, turns, codes, fill_draw, contributions, reg, npatch)
+    got, places, *factor = exchange(slots, turns, codes, still, contributions, reg, npatch)
 
     diag = (patch_id * rowblk + col_id).astype(jnp.int32)[None]
     matrix = place(places, diag, got, reg)
 
-    rows_l, cols_l = spread(fill_draw, matrix, factor, npatch, ncol)
+    rows_l, cols_l = spread(still, matrix, factor, npatch, ncol)
     rows_l = rows_l.reshape(rowblk * width, K * width)
 
     schur, panels = trailing(fill_draw, matrix.reshape(colslots, rowblk * width, width), rows_l, cols_l)

time: 255 us -> 243 us (0.953)
  Pallas kernels: 248 us -> 240 us
  local copies, waits for them, and re-layouts: 3.12 us -> 0.1 us
    pallas_call x1, Pallas kernels: 151 us -> 144 us  [exchange(): pl.pallas_call(functools.partial(exchange_kernel, npatch), in_specs=[SMEM...]
    unnamed x8 -> x4, local copies, waits for them, and re-layouts: 3.04 us -> 0.02 us
where the time goes in v7:
time: 243 us
  Pallas kernels  240 us (99%)
    pallas_call x1, Pallas kernels, exchange(): pl.pallas_call(functools.partial(exchange_kernel, npatch), in_specs=[SMEM...  144 us
    pallas_call x1, Pallas kernels, spread(): pl.pallas_call(spread_kernel, grid=(1,), in_specs=[HBM, pl.BlockSpec((K,)...  68.5 us
    pallas_call x1, Pallas kernels, trailing(): pl.pallas_call(functools.partial(schur_kernel, pair, chunk), grid=(colslo...  19.5 us
    pallas_call x1, Pallas kernels, place(): pl.pallas_call(functools.partial(place_kernel, per, ndevice // per - 1),...  7.76 us

profile of v7, /device:TPU:24, one launch (start us, length us, event | category | flops | bytes accessed | tf_op | source)
XLA Modules:
  0.0 242.6 jit_solution(7894501596885621834)
XLA Ops:
  0.6 0.0 copy-start
  1.3 0.0 copy-done
  1.3 0.1 dynamic-slice_bitcast_fusion.reg_ref
  1.4 0.9 select_reduce_fusion
  2.3 0.1 select_reduce_fusion.1
  2.5 144.2 %exchange.1 = (f32[128,128,128]{2,1,0:T(8,128)}, s32[1,128]{1,0:T(1,128)S(1)}, bf16[8,128,1024]{2,1,0:T(8,128)(2,1)S(1)}, bf16[8,128,1024]{2,1,0:T(8,128)(2,1)S(...) custom-call(s32[128]{0:T(128)S(1)} %get-tuple-element.30.slots, ...), custom_call_target="tpu_custom_call" | custom-call | tf_op jit(solution)/shard_map/exchange/pallas_call | solution.py:740
  146.6 7.8 %place.1.panel_ref = f32[128,128,128]{2,1,0:T(8,128)S(1)} custom-call(s32[1,128]{1,0:T(1,128)S(1)} %get-tuple-element.13.codes, s32[1]{0:T(128)} %bitcast.6.diag, f32[128,128,128]{2,1,0:T(8,128)} %get-tuple-element.14.x_ref, f32[1,128]{1,0:T(1,128)S(1)} %dynamic-slice_bitcast_fusion.reg_ref), custom_call_target="tpu_custom_call" | custom-call | tf_op jit(solution)/shard_map/place/pallas_call | solution.py:73
  154.4 0.0 copy-start.1
  154.4 68.5 %spread.1 = (f32[8,128,1024]{2,1,0:T(8,128)S(1)}, f32[16,128,1024]{2,1,0:T(8,128)S(1)}) custom-call(s32[128,128]{1,0:T(8,128)} %fill.3, f32[128,128,128]{2,1,0:T(8,128)S(1)} %place.1.panel_ref, bf16[8,128,1024]{2,1,0:T(8,128)(2,1)S(1)} %get-tuple-element.15.refs_0_, bf16[8,128,1024]{2,1,0:T(8,128)(2,1)S(1)} %get-tuple-element.16.refs_1_, ...), custom_call_target="tpu_custom_call" | custom-call | tf_op jit(solution)/shard_map/spread/pallas_call | solution.py:455
  222.9 0.0 copy-done.1
  222.9 19.5 %trailing.1 = (f32[16,1024,128]{2,1,0:T(8,128)}, f32[1024,1024]{1,0:T(8,128)}) custom-call(s32[128,128]{1,0:T(8,128)S(1)} %copy-done.1, f32[16,1024,128]{2,1,0:T(8,128)S(1)} %bitcast.18, f32[1024,1024]{1,0:T(8,128)S(1)} %bitcast.19, f32[16,128,1024]{2,1,0:T(8,128)S(1)} %get-tuple-element.21.cols_ref), custom_call_target="tpu_custom_call" | custom-call | tf_op jit(solution)/shard_map/trailing/pallas_call | solution.py:261
  (5 shorter events, 0.0 us)
Async XLA Ops:
  0.6 0.7 copy-start
  154.4 68.5 %copy-start.1 = (s32[128,128]{1,0:T(8,128)S(1)}, s32[128,128]{1,0:T(8,128)}, u32[]{:S(2)}) copy-start(s32[128,128]{1,0:T(8,128)} %fill.3) | copy-start | bytes 196612

commit v8 on v7

--- a/solution.py
+++ b/solution.py
@@ -255,7 +255,7 @@
         pltpu.make_async_copy(rows_ref, panels_ref, sem).wait()
 
 
-def trailing(fill, matrix, rows_l, cols_l, pair=2, chunk=4):
+def trailing(fill, matrix, rows_l, cols_l, pair=2, chunk=8):
     colslots, tall, width = matrix.shape
     depth = rows_l.shape[1]
     return pl.pallas_call(

time: 243 us -> 241 us (level)
  no operation moved by 1% of the time
where the time goes in v8:
time: 241 us
  Pallas kernels  238 us (99%)
    pallas_call x1, Pallas kernels, exchange(): pl.pallas_call(functools.partial(exchange_kernel, npatch), in_specs=[SMEM...  144 us
    pallas_call x1, Pallas kernels, spread(): pl.pallas_call(spread_kernel, grid=(1,), in_specs=[HBM, pl.BlockSpec((K,)...  68.5 us
    pallas_call x1, Pallas kernels, trailing(): pl.pallas_call(functools.partial(schur_kernel, pair, chunk), grid=(colslo...  18 us
    pallas_call x1, Pallas kernels, place(): pl.pallas_call(functools.partial(place_kernel, per, ndevice // per - 1),...  7.75 us

profile of v8, /device:TPU:24, one launch (start us, length us, event | category | flops | bytes accessed | tf_op | source)
XLA Modules:
  0.0 241.1 jit_solution(480064735603859653)
XLA Ops:
  0.6 0.0 copy-start
  1.3 0.0 copy-done
  1.3 0.1 dynamic-slice_bitcast_fusion.reg_ref
  1.4 0.9 select_reduce_fusion
  2.3 0.1 select_reduce_fusion.1
  2.5 144.2 %exchange.1 = (f32[128,128,128]{2,1,0:T(8,128)}, s32[1,128]{1,0:T(1,128)S(1)}, bf16[8,128,1024]{2,1,0:T(8,128)(2,1)S(1)}, bf16[8,128,1024]{2,1,0:T(8,128)(2,1)S(...) custom-call(s32[128]{0:T(128)S(1)} %get-tuple-element.30.slots, ...), custom_call_target="tpu_custom_call" | custom-call | tf_op jit(solution)/shard_map/exchange/pallas_call | solution.py:740
  146.6 7.7 %place.1.panel_ref = f32[128,128,128]{2,1,0:T(8,128)S(1)} custom-call(s32[1,128]{1,0:T(1,128)S(1)} %get-tuple-element.13.codes, s32[1]{0:T(128)} %bitcast.6.diag, f32[128,128,128]{2,1,0:T(8,128)} %get-tuple-element.14.x_ref, f32[1,128]{1,0:T(1,128)S(1)} %dynamic-slice_bitcast_fusion.reg_ref), custom_call_target="tpu_custom_call" | custom-call | tf_op jit(solution)/shard_map/place/pallas_call | solution.py:73
  154.4 0.0 copy-start.1
  154.4 68.5 %spread.1 = (f32[8,128,1024]{2,1,0:T(8,128)S(1)}, f32[16,128,1024]{2,1,0:T(8,128)S(1)}) custom-call(s32[128,128]{1,0:T(8,128)} %fill.3, f32[128,128,128]{2,1,0:T(8,128)S(1)} %place.1.panel_ref, bf16[8,128,1024]{2,1,0:T(8,128)(2,1)S(1)} %get-tuple-element.15.refs_0_, bf16[8,128,1024]{2,1,0:T(8,128)(2,1)S(1)} %get-tuple-element.16.refs_1_, ...), custom_call_target="tpu_custom_call" | custom-call | tf_op jit(solution)/shard_map/spread/pallas_call | solution.py:455
  222.9 0.0 copy-done.1
  222.9 18.0 %trailing.1 = (f32[16,1024,128]{2,1,0:T(8,128)}, f32[1024,1024]{1,0:T(8,128)}) custom-call(s32[128,128]{1,0:T(8,128)S(1)} %copy-done.1, f32[16,1024,128]{2,1,0:T(8,128)S(1)} %bitcast.18, f32[1024,1024]{1,0:T(8,128)S(1)} %bitcast.19, f32[16,128,1024]{2,1,0:T(8,128)S(1)} %get-tuple-element.21.cols_ref), custom_call_target="tpu_custom_call" | custom-call | tf_op jit(solution)/shard_map/trailing/pallas_call | solution.py:261
  (5 shorter events, 0.0 us)
Async XLA Ops:
  0.6 0.7 copy-start
  154.4 68.5 %copy-start.1 = (s32[128,128]{1,0:T(8,128)S(1)}, s32[128,128]{1,0:T(8,128)}, u32[]{:S(2)}) copy-start(s32[128,128]{1,0:T(8,128)} %fill.3) | copy-start | bytes 196612
